TPU v7x, 32 devices: a whole 2x2x4 slice. The times are simulated.
32 devices in a mesh: leaf: 16 (over z, y, x), panel: 2 (over core).
Axes of the slice: x: 2, y: 2, z: 4, core: 2. Of those that a mesh axis runs over, the one named last changes fastest.
Arguments:
- child_front: bfloat16 [4096, 16384], P('leaf', 'panel'), may hold values from -6 to 6
- own_map: int32 [3, 16, 2], P(None, 'leaf'), may hold values from 0 to 1, each once within a row
- cross_map: int32 [3, 16, 2], P(None, 'leaf'), may hold values from 0 to 1, each once within a row
- pivot_inverse: bfloat16 [7, 512, 512], replicated, may hold values from -0.0029296875 to 0.0029296875
Outputs:
- schur: bfloat16 [4096, 16384], P('leaf', 'panel')
Inputs may be any that keep to these rules, and one draw needn't show every extreme that they name: Each own_map[k, d, :] is a permutation of the 2 blocks. Each cross_map[k, d, :] is a permutation of the 2 blocks.
All inputs are finite; a program needn't handle non-finite values.
Results may differ from a plain program's by a relative error of at most 0.0088.
Values may be sent and summed in bfloat16 or wider, within the bound.
No kernel may reach another device: no remote copies, remote signals or barrier semaphores. Data moves between devices by JAX's collectives and lax.ppermute only.
A program may use at most 64 MiB of HBM per device.

v0:
```python
import functools
import math

import jax
import jax.numpy as jnp
from jax import lax
from jax.experimental import pallas as pl
from jax.experimental.pallas import tpu as pltpu
from jax.sharding import PartitionSpec as P


PANEL = 512
BLOCK = 128
MAP_ROWS = 16
MAP_COLS = 12
SHARES = (1, 2, 1)
APART = (2,)
TILE = 256
FINAL_TILE = 512

F32 = jnp.float32
BF16 = jnp.bfloat16


def xor_leaf(block, mask):
    count = lax.axis_size("leaf")
    return lax.ppermute(block, "leaf", [(i, i ^ mask) for i in range(count)])


def xor_panel(block, mask):
    count = lax.axis_size("panel")
    return lax.ppermute(block, "panel", [(i, i ^ mask) for i in range(count)])


def dot(a, b):
    return jnp.dot(a, b, preferred_element_type=F32)


def room(*shapes):
    total = sum(2 * math.prod(shape) for shape in shapes)
    return pltpu.CompilerParams(vmem_limit_bytes=min(total + (6 << 20), 60 << 20))


def vmem():
    return pl.BlockSpec(memory_space=pltpu.VMEM)


def in_hbm(shape):
    return pltpu.HBM(shape, BF16)


def smem():
    return pl.BlockSpec(memory_space=pltpu.SMEM)


def anywhere():
    return pl.BlockSpec(memory_space=pl.ANY)


def block_at(index):
    return pl.ds(pl.multiple_of(index * BLOCK, BLOCK), BLOCK)


def turn(r, meta, count, share):
    return pl.ds(pl.multiple_of(((r ^ meta[0]) & (count - 1)) * share, share), share)


def own_at(level, slot):
    return 2 * level + slot


def cross_at(level, slot):
    return 6 + 2 * level + slot


def lead_level0_kernel(share, meta, maps, *refs):
    parts = refs[:-6]
    inverse, left, seed, near, pivots, sems = refs[-6:]
    group, width = near.shape[0], parts[0].shape[2]
    copies = []
    for i, part in enumerate(parts):
        column = pl.multiple_of((meta[1] ^ i) * width, width)
        source = part.at[:, pl.ds(0, 2 * BLOCK), :]
        copies.append(pltpu.make_async_copy(source, near.at[:, :, pl.ds(column, width)], sems.at[i]))
    for copy in copies:
        copy.start()
    for copy in copies:
        copy.wait()
    rows = 2 * BLOCK
    rest = rows - share
    for r in range(group):
        sibling = r ^ (group // 2)
        for s in range(2):
            own = near[r, block_at(maps[r, own_at(0, s)]), :]
            cross = near[sibling, block_at(maps[r, cross_at(0, s)]), :]
            summed = own + cross
            if s == 0:
                pivots[turn(r, meta, group, share), :] = summed[:share]
                if share < BLOCK:
                    left[r * rest:r * rest + BLOCK - share, :] = summed[share:]
            else:
                left[r * rest + BLOCK - share:(r + 1) * rest, :] = summed
    upper = dot(inverse[0], pivots[...]).astype(BF16)
    mine = left[0:rest, :]
    seed[...] = (mine.astype(F32) - dot(mine, upper)).astype(BF16)


def lead_level12_kernel(gone, share, keep, parts, meta, maps, *refs):
    gathered = refs[:parts]
    inverses = refs[parts:parts + 2]
    left1, left2, front, pivots, upper, sems = refs[parts + 2:]
    group, planes = gathered[0].shape[0], gathered[0].shape[1]
    width = gathered[0].shape[3]
    slabs = group * planes
    rows = 2 * BLOCK
    rest = rows - share
    last = rows - keep
    copies = []
    for i in range(parts):
        column = pl.multiple_of((meta[1] ^ i) * width, width)
        for h in range(planes):
            copy = pltpu.make_async_copy(
                gathered[i].at[:, h, pl.ds(0, rows - gone), :],
                front.at[pl.ds(h * group, group), pl.ds(gone, rows - gone), pl.ds(column, width)],
                sems.at[i * planes + h],
            )
            copy.start()
            copies.append(copy)
    front[:, 0:gone, :] = jnp.zeros((slabs, gone, PANEL), BF16)
    for copy in copies:
        copy.wait()

    def extend1(slab, carry):
        sibling = slab ^ group
        base = slab * rest
        for s in range(2):
            own = front[slab, block_at(maps[slab, own_at(1, s)]), :]
            cross = front[sibling, block_at(maps[slab, cross_at(1, s)]), :]
            summed = own + cross
            if s == 0:
                pivots[slab // (slabs // 2), turn(slab, meta, slabs // 2, share), :] = summed[:share]
                left1[pl.ds(pl.multiple_of(base, 16), BLOCK - share), :] = summed[share:]
            else:
                left1[pl.ds(pl.multiple_of(base + BLOCK - share, 16), BLOCK), :] = summed
        return carry

    lax.fori_loop(0, slabs, extend1, 0)
    for half in range(2):
        upper[...] = dot(inverses[half][0], pivots[half]).astype(BF16)

        def reduce1(pair, carry):
            first = half * (slabs // 2) + 2 * pair
            mine = left1[pl.ds(pl.multiple_of(first * rest, 16), 2 * rest), :]
            reduced = (mine.astype(F32) - dot(mine, upper[...])).astype(BF16)
            front[first, share:rows, :] = reduced[:rest]
            front[first + 1, share:rows, :] = reduced[rest:]
            return carry

        lax.fori_loop(0, slabs // 4, reduce1, 0)

    def extend2(slab, carry):
        sibling = slab + slabs // 2
        base = slab * last
        for s in range(2):
            own = front[slab, block_at(maps[slab, own_at(2, s)]), :]
            cross = front[sibling, block_at(maps[slab, cross_at(2, s)]), :]
            summed = own + cross
            if s == 0:
                left2[pl.ds(pl.multiple_of(base, 16), BLOCK - keep), :] = summed[keep:]
            else:
                left2[pl.ds(pl.multiple_of(base + BLOCK - keep, 16), BLOCK), :] = summed
        return carry

    lax.fori_loop(0, slabs // 2, extend2, 0)


def level0_kernel(share, meta, maps, *refs):
    give, stay, parent, pivots = refs[-4:]
    group = give.shape[0]
    slabs = refs[:group]
    left, inverse = refs[group:group + 2]
    rows = 2 * BLOCK
    rest = rows - share
    for r in range(group):
        sibling = slabs[r ^ (group // 2)]
        for s in range(2):
            own = slabs[r][block_at(maps[r, own_at(0, s)]), :]
            cross = sibling[block_at(maps[r, cross_at(0, s)]), :]
            parent[r, s * BLOCK:(s + 1) * BLOCK, :] = own + cross
        pivots[turn(r, meta, group, share), :] = parent[r, 0:share, :]
    upper = dot(inverse[0], pivots[...]).astype(BF16)
    product = dot(left[...], upper)

    def write(out):
        for r in range(group):
            kept = parent[r, share:rows, :].astype(F32)
            out[r, :, :] = (kept - product[r * rest:(r + 1) * rest]).astype(BF16)

    first = pl.program_id(0) < pl.num_programs(0) // 2
    pl.when(first)(lambda: write(give))
    pl.when(jnp.logical_not(first))(lambda: write(stay))


def level12_kernel(gone, share, final, keep, meta, maps, *refs):
    planes = refs[:4]
    left1_in, left2_in = refs[4:6]
    inverses = refs[6:9]
    outs = refs[9:-9]
    front, parent, nextf, upper, pivots, finals, left1, left2, sems = refs[-9:]
    group = planes[0].shape[0]
    slabs = 4 * group
    tile = planes[0].shape[2]
    rows = 2 * BLOCK
    rest = rows - share
    last = rows - keep

    load1 = pltpu.make_async_copy(left1_in, left1, sems.at[0])
    load2 = pltpu.make_async_copy(left2_in, left2, sems.at[1])
    opening = pl.program_id(0) == 0

    @pl.when(opening)
    def _():
        load1.start()
        load2.start()
        front[:, 0:gone, :] = jnp.zeros((slabs, gone, tile), BF16)
        nextf[:, 0:share, :] = jnp.zeros((slabs, share, tile), BF16)

    for h in range(4):
        front[h * group:(h + 1) * group, gone:rows, :] = planes[h][...]

    def extend1(slab, carry):
        sibling = slab ^ group
        for s in range(2):
            own = front[slab, block_at(maps[slab, own_at(1, s)]), :]
            cross = front[sibling, block_at(maps[slab, cross_at(1, s)]), :]
            parent[slab, s * BLOCK:(s + 1) * BLOCK, :] = own + cross
        taken = parent[slab, 0:share, :]
        pivots[slab // (2 * group), turn(slab, meta, 2 * group, share), :] = taken
        return carry

    lax.fori_loop(0, slabs, extend1, 0)
    pl.when(opening)(load1.wait)
    for half in range(2):
        upper[...] = dot(inverses[half][0], pivots[half]).astype(BF16)

        def reduce1(quad, carry):
            first = half * 2 * group + 4 * quad
            product = dot(left1[pl.ds(pl.multiple_of(first * rest, 16), 4 * rest), :], upper[...])
            for i in range(4):
                kept = parent[first + i, share:rows, :].astype(F32)
                nextf[first + i, share:rows, :] = (kept - product[i * rest:(i + 1) * rest]).astype(BF16)
            return carry

        lax.fori_loop(0, group // 2, reduce1, 0)

    def extend2(slab, carry):
        sibling = slab + 2 * group
        for s in range(2):
            own = nextf[slab, block_at(maps[slab, own_at(2, s)]), :]
            cross = nextf[sibling, block_at(maps[slab, cross_at(2, s)]), :]
            parent[slab, s * BLOCK:(s + 1) * BLOCK, :] = own + cross
        return carry

    lax.fori_loop(0, 2 * group, extend2, 0)
    head = max(final, 16)
    for slab in range(slabs):
        if slab < 2 * group:
            taken = parent[slab, 0:head, :]
        else:
            at = pl.multiple_of(maps[slab, own_at(2, 0)] * BLOCK, BLOCK)
            own = nextf[slab, pl.ds(at, head), :]
            at = pl.multiple_of(maps[slab, cross_at(2, 0)] * BLOCK, BLOCK)
            taken = own + nextf[slab - 2 * group, pl.ds(at, head), :]
        finals[turn(slab, meta, slabs, final), :] = taken.astype(finals.dtype)[:final]
    upper[...] = dot(inverses[2][0], finals[...].astype(BF16)).astype(BF16)
    pl.when(opening)(load2.wait)
    for slab in range(2 * group):
        product = dot(left2[slab * last:(slab + 1) * last, :], upper[...])
        reduced = parent[slab, keep:rows, :].astype(F32) - product
        if keep < final:
            row = lax.broadcasted_iota(jnp.int32, reduced.shape, 0)
            reduced = jnp.where(row >= final - keep, reduced, 0.0)
        if len(outs) == 1:
            outs[0][(slab ^ meta[0]) & (2 * group - 1), :, :] = reduced.astype(BF16)
        else:
            outs[slab][...] = reduced.astype(BF16)


def place_kernel(keep, count, column, meta, *refs):
    pieces, (out, zeros, sems) = refs[:-3], refs[-3:]
    height, side = pieces[0].shape[-2:]
    copies = []
    for i in range(count):
        piece = pieces[0].at[i] if len(pieces[0].shape) == 3 else pieces[i]
        columns = pl.ds(pl.multiple_of(column(i, meta), side), side)
        copies.append(pltpu.make_async_copy(piece, out.at[pl.ds(keep, height), columns], sems.at[i]))
        if keep:
            copies.append(pltpu.make_async_copy(zeros, out.at[pl.ds(0, keep), columns], sems.at[count + i]))
    if keep:
        zeros[...] = jnp.zeros(zeros.shape, BF16)
    for copy in copies:
        copy.start()
    for copy in copies:
        copy.wait()


def chunk_sizes(span):
    unit = span // sum(SHARES)
    return [unit * share for share in SHARES] if unit % (2 * TILE) == 0 else [span]


def on_device(child_front, own_map, cross_map, pivot_inverse):
    leaf_count = lax.axis_size("leaf")
    panel_count = lax.axis_size("panel")
    leaf = lax.axis_index("leaf")
    panel = lax.axis_index("panel")
    rows, cols = child_front.shape
    group = leaf_count // 4
    member = leaf % group
    share0, share1, share2 = (PANEL // (group << k) for k in range(3))
    keep = share2 // 16 * 16
    span = cols // group
    sizes = chunk_sizes(span)
    starts = [sum(sizes[:k]) for k in range(len(sizes))]
    meta = jnp.stack([leaf, panel]).astype(jnp.int32)
    child_columns = pltpu.with_memory_space_constraint(child_front, pltpu.HBM)
    plane_bits = group.bit_length() - 1

    maps = jnp.concatenate([own_map[:, 0, :], cross_map[:, 0, :]], axis=0).reshape(1, MAP_COLS)
    map_rows = jnp.pad(maps.astype(BF16), ((0, MAP_ROWS - 1), (0, PANEL - MAP_COLS)))
    width = PANEL // panel_count
    part = child_front[:, :width]
    for p in range(1, panel_count):
        copied = lax.ppermute(child_front[:, p * width:(p + 1) * width], "panel", [(0, p)])
        part = jnp.where(panel == p, copied, part)
    part = jnp.concatenate([part, map_rows[:, :width]], axis=0)
    near = jnp.stack([part] + [xor_leaf(part, r) for r in range(1, group)])
    near_maps = near[:, rows, :MAP_COLS].astype(jnp.int32)
    near = [near] + [xor_panel(near, i) for i in range(1, panel_count)]

    received = []
    for k, chunk in enumerate(sizes):
        parts = []
        for r in range(1, group):
            start = (member ^ r) * span + starts[k]
            columns = lax.dynamic_slice(child_front, (0, start), (rows, chunk))
            parts.append(xor_leaf(columns, r))
        received.append(parts)

    rest0, rest1, last = rows - share0, rows - share1, rows - keep

    def inverse_of(front):
        return pl.BlockSpec((1, PANEL, PANEL), lambda j, meta, maps: (front(meta[0] >> plane_bits), 0, 0))

    level1_inverses = [inverse_of(lambda p: 4 + (p >> 1)), inverse_of(lambda p: 5 - (p >> 1))]
    left0, seed = pl.pallas_call(
        functools.partial(lead_level0_kernel, share0),
        out_shape=(
            jax.ShapeDtypeStruct((group * rest0, PANEL), BF16),
            jax.ShapeDtypeStruct((rest0, PANEL), BF16),
        ),
        grid_spec=pltpu.PrefetchScalarGridSpec(
            num_scalar_prefetch=2,
            grid=(1,),
            in_specs=[anywhere()] * panel_count + [inverse_of(lambda p: p)],
            out_specs=(vmem(), vmem()),
            scratch_shapes=[
                pltpu.VMEM((group, rows, PANEL), BF16),
                pltpu.VMEM((PANEL, PANEL), BF16),
                pltpu.SemaphoreType.DMA((panel_count,)),
            ],
        ),
        compiler_params=room((group, rows, PANEL), (group * rest0, PANEL), *[(PANEL, PANEL)] * 4),
        name="lead0",
    )(meta, near_maps, *near, pivot_inverse)

    piece = lax.dynamic_slice(seed, (0, panel * width), (rest0, width))
    piece = jnp.concatenate([piece, map_rows[:, :width]], axis=0)
    piece = jnp.stack([piece] + [xor_leaf(piece, m * group) for m in range(1, 4)])
    piece = jnp.stack([piece] + [xor_leaf(piece, r) for r in range(1, group)])
    gathered = [piece]
    for i in range(1, panel_count):
        gathered.append(xor_panel(piece, i))
    all_maps = piece[:, :, rest0, :MAP_COLS].transpose(1, 0, 2).reshape(leaf_count, MAP_COLS)
    all_maps = all_maps.astype(jnp.int32)

    left1, left2 = pl.pallas_call(
        functools.partial(lead_level12_kernel, share0, share1, keep, panel_count),
        out_shape=(
            jax.ShapeDtypeStruct((leaf_count * rest1, PANEL), BF16),
            jax.ShapeDtypeStruct((2 * group * last, PANEL), BF16),
        ),
        grid_spec=pltpu.PrefetchScalarGridSpec(
            num_scalar_prefetch=2,
            grid=(1,),
            in_specs=[anywhere()] * panel_count + level1_inverses,
            out_specs=(vmem(), vmem()),
            scratch_shapes=[
                pltpu.VMEM((leaf_count, rows, PANEL), BF16),
                pltpu.VMEM((2, PANEL, PANEL), BF16),
                pltpu.VMEM((PANEL, PANEL), BF16),
                pltpu.SemaphoreType.DMA((4 * panel_count,)),
            ],
        ),
        compiler_params=room(
            (leaf_count * (rows + rest1) + 2 * group * last, PANEL), *[(PANEL, PANEL)] * 7
        ),
        name="lead12",
    )(meta, all_maps, *gathered, pivot_inverse, pivot_inverse)

    def level0(k):
        side = sizes[k] // 2
        tile = min(TILE, side)
        count = side // tile

        def column(j, meta):
            odd = (meta[0] >> plane_bits) & 1
            return jnp.where(j < count, (1 - odd) * count + j, odd * count + j - count)

        def own_column(j, meta, maps):
            base = (meta[0] & (group - 1)) * (span // tile) + starts[k] // tile
            return 0, base + column(j, meta)

        return pl.pallas_call(
            functools.partial(level0_kernel, share0),
            out_shape=[jax.ShapeDtypeStruct((group, rest0, side), BF16)] * 2,
            grid_spec=pltpu.PrefetchScalarGridSpec(
                num_scalar_prefetch=2,
                grid=(2 * count,),
                in_specs=[pl.BlockSpec((rows, tile), own_column)]
                + [pl.BlockSpec((rows, tile), lambda j, meta, maps: (0, column(j, meta)))] * (group - 1)
                + [
                    pl.BlockSpec((group * rest0, PANEL), lambda j, meta, maps: (0, 0)),
                    inverse_of(lambda p: p),
                ],
                out_specs=[
                    pl.BlockSpec((group, rest0, tile), lambda j, meta, maps: (0, 0, jnp.minimum(j, count - 1))),
                    pl.BlockSpec((group, rest0, tile), lambda j, meta, maps: (0, 0, jnp.maximum(j - count, 0))),
                ],
                scratch_shapes=[pltpu.VMEM((group, rows, tile), BF16), pltpu.VMEM((PANEL, tile), BF16)],
            ),
            compiler_params=room(
                (7 * group * rows, tile), (2 * group * rest0, PANEL), *[(PANEL, PANEL)] * 2, (PANEL, 4 * tile)
            ),
            name="level0",
        )(meta, near_maps, child_columns, *received[k], left0, pivot_inverse)

    def level12(planes, apart):
        side = planes[0].shape[2]
        tile = min(FINAL_TILE, side)
        return pl.pallas_call(
            functools.partial(level12_kernel, share0, share1, share2, keep),
            out_shape=[in_hbm((last, side))] * (2 * group) if apart else [in_hbm((2 * group, last, side))],
            grid_spec=pltpu.PrefetchScalarGridSpec(
                num_scalar_prefetch=2,
                grid=(side // tile,),
                in_specs=[pl.BlockSpec((group, rest0, tile), lambda j, meta, maps: (0, 0, j))] * 4
                + [anywhere()] * 2
                + level1_inverses
                + [inverse_of(lambda p: 6)],
                out_specs=[pl.BlockSpec((last, tile), lambda j, meta, maps: (0, j))] * (2 * group)
                if apart
                else [pl.BlockSpec((2 * group, last, tile), lambda j, meta, maps: (0, 0, j))],
                scratch_shapes=[
                    pltpu.VMEM((leaf_count, rows, tile), BF16),
                    pltpu.VMEM((leaf_count, rows, tile), BF16),
                    pltpu.VMEM((leaf_count, rows, tile), BF16),
                    pltpu.VMEM((PANEL, tile), BF16),
                    pltpu.VMEM((2, PANEL, tile), BF16),
                    pltpu.VMEM((PANEL, tile), BF16 if share2 % 16 == 0 else F32),
                    pltpu.VMEM((leaf_count * rest1, PANEL), BF16),
                    pltpu.VMEM((2 * group * last, PANEL), BF16),
                    pltpu.SemaphoreType.DMA((2,)),
                ],
            ),
            compiler_params=room(
                (3 * leaf_count * rows + 8 * group * rest0 + 4 * group * last, tile),
                (leaf_count * rest1 + 2 * group * last, PANEL),
                *[(PANEL, PANEL)] * 6,
                (16 * PANEL, tile),
            ),
            name="level12",
        )(meta, all_maps, *planes, left1, left2, *[pivot_inverse] * 3)

    def place(k, pieces, slab):
        side = sizes[k] // 2
        whole = [] if slab is None else [slab]

        def column(i, meta):
            source = i if len(pieces) == 1 else meta[0] ^ i
            odd = (source >> plane_bits) & 1
            return (source & (group - 1)) * span + starts[k] + odd * side

        return pl.pallas_call(
            functools.partial(place_kernel, keep, 2 * group, column),
            out_shape=jax.ShapeDtypeStruct((rows, cols), BF16),
            in_specs=[smem()] + [vmem()] * len(pieces) + [anywhere()] * len(whole),
            out_specs=anywhere(),
            scratch_shapes=[
                pltpu.VMEM((max(keep, 16), side), BF16),
                pltpu.SemaphoreType.DMA((4 * group,)),
            ],
            input_output_aliases={1 + len(pieces): 0} if whole else {},
            compiler_params=room((2 * group, last, side), (max(keep, 16), side)),
            name="place",
        )(meta, *pieces, *whole)

    pairs = [[base + i for i in range(2 * group)] for base in (0, 2 * group)]
    slab = None
    for k in range(len(sizes)):
        give, stay = level0(k)
        from1, from3 = (xor_leaf(give, m * group) for m in (1, 3))
        from2 = xor_leaf(stay, 2 * group)
        apart = k in APART
        done = level12([stay, from1, from2, from3], apart)
        if apart:
            pieces = [done[0]] + [xor_leaf(done[r], r) for r in range(1, 2 * group)]
        else:
            pieces = [lax.all_to_all(done[0], "leaf", 0, 0, axis_index_groups=pairs, tiled=True)]
        slab = place(k, pieces, slab)
    return slab


def solution(mesh):
    placed = (P("leaf", "panel"), P(None, "leaf", None), P(None, "leaf", None), P())
    return jax.shard_map(on_device, mesh=mesh, in_specs=placed, out_specs=P("leaf", "panel"), check_vma=False)
```

profile of v0, /device:TPU:0, one launch (start us, length us, event | category | flops | bytes accessed | tf_op | source)
XLA Modules:
  0.0 295.7 jit_solution(9841835521749334601)
XLA Ops:
  0.9 2.4 collective-permute-start
  4.3 0.9 slice_select_fusion
  5.3 3.3 %collective-permute-start.3 = (bf16[272,256]{1,0:T(8,128)(2,1)S(1)}, bf16[272,256]{1,0:T(8,128)(2,1)S(1)}, u32[]{:S(2)}, u32[]{:S(2)}) collective-permute-start(bf16[272,256]{1,0:T(8,128)(2,1)S(1)} %get-tuple-element.53), channel_id=1, source_target_pairs={{0,6},{2,4},{4,2},{6,0},{8,14},{10,12},{12,10},{14,8},{16,22},{18,... | collective-permute-start | bytes 417800 | tf_op jit(solution)/shard_map/ppermute | solution.py:27
  9.3 3.9 %collective-permute-done.3 = bf16[272,256]{1,0:T(8,128)(2,1)S(1)} collective-permute-done((bf16[272,256]{1,0:T(8,128)(2,1)S(1)}, bf16[272,256]{1,0:T(8,128)(2,1)S(1)}, u32[]{:S(2)}, u32[]{:S(2)}) %collective-permute-start.3) | collective-permute-done | bytes 139296 | tf_op jit(solution)/shard_map/ppermute | solution.py:27
  13.1 2.6 collective-permute-done.2
  16.3 1.9 collective-permute-done.4.refs_1_
  18.2 2.0 copy-done
  20.2 1.4 lead0.1
  21.7 3.7 %collective-permute-start.7 = (bf16[144,256]{1,0:T(8,128)(2,1)S(1)}, bf16[144,256]{1,0:T(8,128)(2,1)S(1)}, u32[]{:S(2)}, u32[]{:S(2)}) collective-permute-start(bf16[144,256]{1,0:T(8,128)(2,1)S(1)} %get-tuple-element.55), channel_id=1, source_target_pairs={{0,24},{2,26},{4,28},{6,30},{8,16},{10,18},{12,20},{14,22},{16,8},... | collective-permute-start | bytes 221192 | tf_op jit(solution)/shard_map/ppermute | solution.py:27
  26.1 2.2 collective-permute-done.7
  28.3 3.6 %collective-permute-done.6 = bf16[144,256]{1,0:T(8,128)(2,1)S(1)} collective-permute-done((bf16[144,256]{1,0:T(8,128)(2,1)S(1)}, bf16[144,256]{1,0:T(8,128)(2,1)S(1)}, u32[]{:S(2)}, u32[]{:S(2)}) %collective-permute-start.6) | collective-permute-done | bytes 73760 | tf_op jit(solution)/shard_map/ppermute | solution.py:27
  31.9 1.7 collective-permute-start.10
  33.6 1.3 collective-permute-start.9
  35.4 7.3 %collective-permute-done.10 = bf16[4,144,256]{2,1,0:T(8,128)(2,1)S(1)} collective-permute-done((bf16[4,144,256]{2,1,0:T(8,128)(2,1)S(1)}, bf16[4,144,256]{2,1,0:T(8,128)(2,1)S(1)}, u32[]{:S(2)}, u32[]{:S(2)}) %collective-permute-start.10) | collective-permute-done | bytes 294944 | tf_op jit(solution)/shard_map/ppermute | solution.py:27
  42.8 4.8 %collective-permute-done.9 = bf16[4,144,256]{2,1,0:T(8,128)(2,1)S(1)} collective-permute-done((bf16[4,144,256]{2,1,0:T(8,128)(2,1)S(1)}, bf16[4,144,256]{2,1,0:T(8,128)(2,1)S(1)}, u32[]{:S(2)}, u32[]{:S(2)}) %collective-permute-start.9) | collective-permute-done | bytes 294944 | tf_op jit(solution)/shard_map/ppermute | solution.py:27
  47.8 2.6 constant_dynamic-slice_fusion
  50.4 1.5 collective-permute-start.31
  52.6 1.3 collective-permute-start.33
  53.9 5.7 %collective-permute-done.31.refs_1_ = bf16[256,512]{1,0:T(8,128)(2,1)S(1)} collective-permute-done((bf16[256,512]{1,0:T(8,128)(2,1)S(1)}, bf16[256,512]{1,0:T(8,128)(2,1)S(1)}, u32[]{:S(2)}, u32[]{:S(2)}) %collective-permute-start.31) | collective-permute-done | bytes 262176 | tf_op jit(solution)/shard_map/ppermute | solution.py:27
  59.6 6.0 %collective-permute-done.32.refs_2_ = bf16[256,512]{1,0:T(8,128)(2,1)S(1)} collective-permute-done((bf16[256,512]{1,0:T(8,128)(2,1)S(1)}, bf16[256,512]{1,0:T(8,128)(2,1)S(1)}, u32[]{:S(2)}, u32[]{:S(2)}) %collective-permute-start.32) | collective-permute-done | bytes 262176 | tf_op jit(solution)/shard_map/ppermute | solution.py:27
  65.6 2.0 copy-done.1
  67.6 3.6 %level0.5 = (bf16[4,128,256]{2,1,0:T(8,128)(2,1)S(1)}, bf16[4,128,256]{2,1,0:T(8,128)(2,1)S(1)}) custom-call(s32[2]{0:T(128)S(1)} %pad_add_fusion.meta, s32[4,12]{1,0:T(4,128)S(1)} %bitcast.31, bf16[256,8192]{1,0:T(8,128)(2,1)} %refs_0_.5, bf16[256,512]{1,0:T(8,128)(2,1)S(1)} %collective-permute-done.31.refs_1_, ...), custom_call_target="tpu_custom_call" | custom-call | tf_op jit(solution)/shard_map/level0/pallas_call | solution.py:424
  71.8 2.5 collective-permute-start.35
  74.3 1.3 collective-permute-start.36
  75.7 1.0 copy-done.15
  76.7 1.3 copy-done.11
  78.0 1.3 copy-done.16
  79.3 5.7 %lead12.1 = (bf16[3072,512]{1,0:T(8,128)(2,1)S(1)}, bf16[1792,512]{1,0:T(8,128)(2,1)S(1)}) custom-call(s32[2]{0:T(128)S(1)} %pad_add_fusion.meta, s32[16,12]{1,0:T(8,128)S(1)} %bitcast.26, bf16[4,4,144,256]{3,2,1,0:T(8,128)(2,1)S(1)} %copy-done.11, bf16[4,4,144,256]{3,2,1,0:T(8,128)(2,1)S(1)} %copy-done.16, bf16[7,512,512]{2,1,0:T(8,128)(2,1)S(1)} %copy-done.2, ...), custom_call_target="tpu_custom_call" | custom-call | tf_op jit(solution)/shard_map/lead12/pallas_call | solution.py:387
  85.0 8.1 %collective-permute-done.35.refs_2_ = bf16[4,128,256]{2,1,0:T(8,128)(2,1)S(1)} collective-permute-done((bf16[4,128,256]{2,1,0:T(8,128)(2,1)S(1)}, bf16[4,128,256]{2,1,0:T(8,128)(2,1)S(1)}, u32[]{:S(2)}, u32[]{:S(2)}) %collective-permute-start.35) | collective-permute-done | bytes 262176 | tf_op jit(solution)/shard_map/ppermute | solution.py:27
  93.1 6.0 %level12.5 = bf16[8,224,256]{2,1,0:T(8,128)(2,1)} custom-call(s32[2]{0:T(128)S(1)} %pad_add_fusion.meta, s32[16,12]{1,0:T(8,128)S(1)} %bitcast.27, bf16[4,128,256]{2,1,0:T(8,128)(2,1)S(1)} %get-tuple-element.39.refs_0_, bf16[4,128,256]{2,1,0:T(8,128)(2,1)S(1)} %collective-permute-done.34.refs_1_, bf16[4,128,256]{2,1,0:T(8,128)(2,1)S(1)} %collective-permute-done.35.refs_2_, ...), custom_call_target="tpu_custom_call" | custom-call | tf_op jit(solution)/shard_map/level12/pallas_call | solution.py:451
  99.1 1.2 copy-done.7
  100.3 6.2 %all-to-all-start.1 = ((bf16[8,224,256]{2,1,0:T(8,128)(2,1)}), bf16[8,224,256]{2,1,0:T(8,128)(2,1)}, u32[]{:S(2)}, u32[]{:S(2)}) async-start(bf16[8,224,256]{2,1,0:T(8,128)(2,1)} %level12.5), calls=%async_computation.1 | async-start | bytes 1835008 | tf_op jit(solution)/shard_map/all_to_all | solution.py:519
  106.6 1.5 constant_dynamic-slice_fusion.3
  108.1 2.1 collective-permute-start.25
  110.2 1.5 collective-permute-start.26
  111.7 18.6 %collective-permute-done.25.refs_1_ = bf16[256,1024]{1,0:T(8,128)(2,1)S(1)} collective-permute-done((bf16[256,1024]{1,0:T(8,128)(2,1)S(1)}, bf16[256,1024]{1,0:T(8,128)(2,1)S(1)}, u32[]{:S(2)}, u32[]{:S(2)}) %collective-permute-start.25) | collective-permute-done | bytes 524320 | tf_op jit(solution)/shard_map/ppermute | solution.py:27
  131.1 9.2 %collective-permute-done.27.refs_3_ = bf16[256,1024]{1,0:T(8,128)(2,1)S(1)} collective-permute-done((bf16[256,1024]{1,0:T(8,128)(2,1)S(1)}, bf16[256,1024]{1,0:T(8,128)(2,1)S(1)}, u32[]{:S(2)}, u32[]{:S(2)}) %collective-permute-start.27) | collective-permute-done | bytes 524320 | tf_op jit(solution)/shard_map/ppermute | solution.py:27
  140.3 2.0 copy-done.3
  142.4 5.6 %level0.4 = (bf16[4,128,512]{2,1,0:T(8,128)(2,1)S(1)}, bf16[4,128,512]{2,1,0:T(8,128)(2,1)S(1)}) custom-call(s32[2]{0:T(128)S(1)} %pad_add_fusion.meta, s32[4,12]{1,0:T(4,128)S(1)} %bitcast.32, bf16[256,8192]{1,0:T(8,128)(2,1)} %refs_0_.5, bf16[256,1024]{1,0:T(8,128)(2,1)S(1)} %collective-permute-done.25.refs_1_, ...), custom_call_target="tpu_custom_call" | custom-call | tf_op jit(solution)/shard_map/level0/pallas_call | solution.py:424
  148.0 1.5 collective-permute-start.28
  149.5 3.2 %collective-permute-start.29 = (bf16[4,128,512]{2,1,0:T(8,128)(2,1)S(1)}, bf16[4,128,512]{2,1,0:T(8,128)(2,1)S(1)}, u32[]{:S(2)}, u32[]{:S(2)}) collective-permute-start(bf16[4,128,512]{2,1,0:T(8,128)(2,1)S(1)} %get-tuple-element.37.refs_0_), channel_id=1, source_target_pairs={{0,16},{2,18},{4,20},{6,22},{8,24},{10,26},{12,28},{14,30},{16,0},... | collective-permute-start | bytes 1572872 | tf_op jit(solution)/shard_map/ppermute | solution.py:27
  152.7 17.4 %collective-permute-done.28.refs_1_ = bf16[4,128,512]{2,1,0:T(8,128)(2,1)S(1)} collective-permute-done((bf16[4,128,512]{2,1,0:T(8,128)(2,1)S(1)}, bf16[4,128,512]{2,1,0:T(8,128)(2,1)S(1)}, u32[]{:S(2)}, u32[]{:S(2)}) %collective-permute-start.28) | collective-permute-done | bytes 524320 | tf_op jit(solution)/shard_map/ppermute | solution.py:27
  170.1 17.8 %collective-permute-done.29.refs_2_ = bf16[4,128,512]{2,1,0:T(8,128)(2,1)S(1)} collective-permute-done((bf16[4,128,512]{2,1,0:T(8,128)(2,1)S(1)}, bf16[4,128,512]{2,1,0:T(8,128)(2,1)S(1)}, u32[]{:S(2)}, u32[]{:S(2)}) %collective-permute-start.29) | collective-permute-done | bytes 524320 | tf_op jit(solution)/shard_map/ppermute | solution.py:27
  187.9 8.3 %level12.4 = bf16[8,224,512]{2,1,0:T(8,128)(2,1)} custom-call(s32[2]{0:T(128)S(1)} %pad_add_fusion.meta, s32[16,12]{1,0:T(8,128)S(1)} %bitcast.28, bf16[4,128,512]{2,1,0:T(8,128)(2,1)S(1)} %get-tuple-element.37.refs_0_, bf16[4,128,512]{2,1,0:T(8,128)(2,1)S(1)} %collective-permute-done.28.refs_1_, bf16[4,128,512]{2,1,0:T(8,128)(2,1)S(1)} %collective-permute-done.29.refs_2_, ...), custom_call_target="tpu_custom_call" | custom-call | tf_op jit(solution)/shard_map/level12/pallas_call | solution.py:451
  196.2 11.2 %all-to-all-start = ((bf16[8,224,512]{2,1,0:T(8,128)(2,1)}), bf16[8,224,512]{2,1,0:T(8,128)(2,1)}, u32[]{:S(2)}, u32[]{:S(2)}) async-start(bf16[8,224,512]{2,1,0:T(8,128)(2,1)} %level12.4), calls=%async_computation | async-start | bytes 3670016 | tf_op jit(solution)/shard_map/all_to_all | solution.py:519
  207.5 2.0 collective-permute-start.11
  209.5 1.5 collective-permute-start.12
  211.0 25.3 %collective-permute-done.11.refs_1_ = bf16[256,512]{1,0:T(8,128)(2,1)S(1)} collective-permute-done((bf16[256,512]{1,0:T(8,128)(2,1)}, bf16[256,512]{1,0:T(8,128)(2,1)S(1)}, u32[]{:S(2)}, u32[]{:S(2)}) %collective-permute-start.11) | collective-permute-done | bytes 262176 | tf_op jit(solution)/shard_map/ppermute | solution.py:27
  236.3 4.2 %collective-permute-done.13.refs_3_ = bf16[256,512]{1,0:T(8,128)(2,1)S(1)} collective-permute-done((bf16[256,512]{1,0:T(8,128)(2,1)S(1)}, bf16[256,512]{1,0:T(8,128)(2,1)S(1)}, u32[]{:S(2)}, u32[]{:S(2)}) %collective-permute-start.13) | collective-permute-done | bytes 262176 | tf_op jit(solution)/shard_map/ppermute | solution.py:27
  240.5 2.0 copy-done.5
  242.5 1.0 copy-done.14
  243.6 3.5 %level0.3 = (bf16[4,128,256]{2,1,0:T(8,128)(2,1)S(1)}, bf16[4,128,256]{2,1,0:T(8,128)(2,1)S(1)}) custom-call(s32[2]{0:T(128)S(1)} %pad_add_fusion.meta, s32[4,12]{1,0:T(4,128)S(1)} %bitcast.33, bf16[256,8192]{1,0:T(8,128)(2,1)} %refs_0_.5, bf16[256,512]{1,0:T(8,128)(2,1)S(1)} %collective-permute-done.11.refs_1_, ...), custom_call_target="tpu_custom_call" | custom-call | tf_op jit(solution)/shard_map/level0/pallas_call | solution.py:424
  247.1 0.9 collective-permute-start.14
  248.1 3.2 %collective-permute-start.15 = (bf16[4,128,256]{2,1,0:T(8,128)(2,1)S(1)}, bf16[4,128,256]{2,1,0:T(8,128)(2,1)S(1)}, u32[]{:S(2)}, u32[]{:S(2)}) collective-permute-start(bf16[4,128,256]{2,1,0:T(8,128)(2,1)S(1)} %get-tuple-element.25.refs_0_), channel_id=1, source_target_pairs={{0,16},{2,18},{4,20},{6,22},{8,24},{10,26},{12,28},{14,30},{16,0},... | collective-permute-start | bytes 786440 | tf_op jit(solution)/shard_map/ppermute | solution.py:27
  252.0 7.6 %collective-permute-done.14.refs_1_ = bf16[4,128,256]{2,1,0:T(8,128)(2,1)S(1)} collective-permute-done((bf16[4,128,256]{2,1,0:T(8,128)(2,1)S(1)}, bf16[4,128,256]{2,1,0:T(8,128)(2,1)S(1)}, u32[]{:S(2)}, u32[]{:S(2)}) %collective-permute-start.14) | collective-permute-done | bytes 262176 | tf_op jit(solution)/shard_map/ppermute | solution.py:27
  259.6 10.0 %collective-permute-done.15.refs_2_ = bf16[4,128,256]{2,1,0:T(8,128)(2,1)S(1)} collective-permute-done((bf16[4,128,256]{2,1,0:T(8,128)(2,1)S(1)}, bf16[4,128,256]{2,1,0:T(8,128)(2,1)S(1)}, u32[]{:S(2)}, u32[]{:S(2)}) %collective-permute-start.15) | collective-permute-done | bytes 262176 | tf_op jit(solution)/shard_map/ppermute | solution.py:27
  269.6 5.7 %level12.3 = (bf16[224,256]{1,0:T(8,128)(2,1)}, bf16[224,256]{1,0:T(8,128)(2,1)}, bf16[224,256]{1,0:T(8,128)(2,1)}, bf16[224,256]{1,0:T(8,128)(2,1)}, bf16[224,2...) custom-call(s32[2]{0:T(128)S(1)} %pad_add_fusion.meta, ...), custom_call_target="tpu_custom_call" | custom-call | tf_op jit(solution)/shard_map/level12/pallas_call | solution.py:451
  275.4 2.3 collective-permute-start.18
  279.2 4.4 %collective-permute-start.21 = (bf16[224,256]{1,0:T(8,128)(2,1)}, bf16[224,256]{1,0:T(8,128)(2,1)S(1)}, u32[]{:S(2)}, u32[]{:S(2)}) collective-permute-start(bf16[224,256]{1,0:T(8,128)(2,1)} %get-tuple-element.33), channel_id=1, source_target_pairs={{0,8},{2,10},{4,12},{6,14},{8,0},{10,2},{12,4},{14,6},{16,24},{18,... | collective-permute-start | bytes 344072 | tf_op jit(solution)/shard_map/ppermute | solution.py:27
  283.6 1.4 collective-permute-start.22
  285.0 2.1 collective-permute-start.23
  288.0 2.3 place.3.refs_1_
  290.3 3.0 %place.4.refs_8_ = bf16[256,8192]{1,0:T(8,128)(2,1)} custom-call(s32[2]{0:T(128)S(1)} %pad_add_fusion.meta, bf16[8,224,512]{2,1,0:T(8,128)(2,1)} %all-to-all-done.refs_0_, bf16[256,8192]{1,0:T(8,128)(2,1)} %place.3.refs_1_), custom_call_target="tpu_custom_call", output_to_operand_aliasing={{}: (2, {})} | custom-call | tf_op jit(solution)/shard_map/place/pallas_call | solution.py:494
  293.9 1.6 place.5
  (80 shorter events, 10.9 us)
Async XLA Ops:
  0.9 3.4 %collective-permute-start = (bf16[256,256]{1,0:T(8,128)(2,1)S(1)}, bf16[256,256]{1,0:T(8,128)(2,1)S(1)}, u32[]{:S(2)}, u32[]{:S(2)}) collective-permute-start(bf16[256,256]{1,0:T(8,128)(2,1)S(1)} %slice.16), channel_id=1, source_target_pairs={{0,1},{2,3},{4,5},{6,7},{8,9},{10,11},{12,13},{14,15},{16,17},{18,... | collective-permute-start | bytes 393224 | tf_op jit(solution)/shard_map/ppermute | solution.py:334
  5.3 7.8 %collective-permute-start.3 = (bf16[272,256]{1,0:T(8,128)(2,1)S(1)}, bf16[272,256]{1,0:T(8,128)(2,1)S(1)}, u32[]{:S(2)}, u32[]{:S(2)}) collective-permute-start(bf16[272,256]{1,0:T(8,128)(2,1)S(1)} %get-tuple-element.53), channel_id=1, source_target_pairs={{0,6},{2,4},{4,2},{6,0},{8,14},{10,12},{12,10},{14,8},{16,22},{18,... | collective-permute-start | bytes 417800 | tf_op jit(solution)/shard_map/ppermute | solution.py:27
  8.6 7.1 %collective-permute-start.2 = (bf16[272,256]{1,0:T(8,128)(2,1)S(1)}, bf16[272,256]{1,0:T(8,128)(2,1)S(1)}, u32[]{:S(2)}, u32[]{:S(2)}) collective-permute-start(bf16[272,256]{1,0:T(8,128)(2,1)S(1)} %get-tuple-element.53), channel_id=1, source_target_pairs={{0,4},{2,6},{4,0},{6,2},{8,12},{10,14},{12,8},{14,10},{16,20},{18,... | collective-permute-start | bytes 417800 | tf_op jit(solution)/shard_map/ppermute | solution.py:27
  9.1 6.9 %collective-permute-start.1 = (bf16[272,256]{1,0:T(8,128)(2,1)S(1)}, bf16[272,256]{1,0:T(8,128)(2,1)S(1)}, u32[]{:S(2)}, u32[]{:S(2)}) collective-permute-start(bf16[272,256]{1,0:T(8,128)(2,1)S(1)} %get-tuple-element.53), channel_id=1, source_target_pairs={{0,2},{2,0},{4,6},{6,4},{8,10},{10,8},{12,14},{14,12},{16,18},{18,... | collective-permute-start | bytes 417800 | tf_op jit(solution)/shard_map/ppermute | solution.py:27
  16.1 2.0 collective-permute-start.4
  18.1 2.0 copy-start
  21.6 44.0 %copy-start.12 = (bf16[512,512]{1,0:T(8,128)(2,1)}, bf16[512,512]{1,0:T(8,128)(2,1)S(1)}, u32[]{:S(2)}) copy-start(bf16[512,512]{1,0:T(8,128)(2,1)S(1)} %get-tuple-element.24.refs_4_) | copy-start | bytes 1572868
  21.7 6.6 %collective-permute-start.7 = (bf16[144,256]{1,0:T(8,128)(2,1)S(1)}, bf16[144,256]{1,0:T(8,128)(2,1)S(1)}, u32[]{:S(2)}, u32[]{:S(2)}) collective-permute-start(bf16[144,256]{1,0:T(8,128)(2,1)S(1)} %get-tuple-element.55), channel_id=1, source_target_pairs={{0,24},{2,26},{4,28},{6,30},{8,16},{10,18},{12,20},{14,22},{16,8},... | collective-permute-start | bytes 221192 | tf_op jit(solution)/shard_map/ppermute | solution.py:27
  25.3 6.5 %collective-permute-start.6 = (bf16[144,256]{1,0:T(8,128)(2,1)S(1)}, bf16[144,256]{1,0:T(8,128)(2,1)S(1)}, u32[]{:S(2)}, u32[]{:S(2)}) collective-permute-start(bf16[144,256]{1,0:T(8,128)(2,1)S(1)} %get-tuple-element.55), channel_id=1, source_target_pairs={{0,16},{2,18},{4,20},{6,22},{8,24},{10,26},{12,28},{14,30},{16,0},... | collective-permute-start | bytes 221192 | tf_op jit(solution)/shard_map/ppermute | solution.py:27
  25.3 6.5 %collective-permute-start.5 = (bf16[144,256]{1,0:T(8,128)(2,1)S(1)}, bf16[144,256]{1,0:T(8,128)(2,1)S(1)}, u32[]{:S(2)}, u32[]{:S(2)}) collective-permute-start(bf16[144,256]{1,0:T(8,128)(2,1)S(1)} %get-tuple-element.55), channel_id=1, source_target_pairs={{0,8},{2,10},{4,12},{6,14},{8,0},{10,2},{12,4},{14,6},{16,24},{18,... | collective-permute-start | bytes 221192 | tf_op jit(solution)/shard_map/ppermute | solution.py:27
  31.9 10.9 %collective-permute-start.10 = (bf16[4,144,256]{2,1,0:T(8,128)(2,1)S(1)}, bf16[4,144,256]{2,1,0:T(8,128)(2,1)S(1)}, u32[]{:S(2)}, u32[]{:S(2)}) collective-permute-start(bf16[4,144,256]{2,1,0:T(8,128)(2,1)S(1)} %get-tuple-element.51), channel_id=1, source_target_pairs={{0,6},{2,4},{4,2},{6,0},{8,14},{10,12},{12,10},{14,8},{16,22},{18,... | collective-permute-start | bytes 884744 | tf_op jit(solution)/shard_map/ppermute | solution.py:27
  33.6 13.9 %collective-permute-start.9 = (bf16[4,144,256]{2,1,0:T(8,128)(2,1)S(1)}, bf16[4,144,256]{2,1,0:T(8,128)(2,1)S(1)}, u32[]{:S(2)}, u32[]{:S(2)}) collective-permute-start(bf16[4,144,256]{2,1,0:T(8,128)(2,1)S(1)} %get-tuple-element.51), channel_id=1, source_target_pairs={{0,4},{2,6},{4,0},{6,2},{8,12},{10,14},{12,8},{14,10},{16,20},{18,... | collective-permute-start | bytes 884744 | tf_op jit(solution)/shard_map/ppermute | solution.py:27
  34.9 12.6 %collective-permute-start.8 = (bf16[4,144,256]{2,1,0:T(8,128)(2,1)S(1)}, bf16[4,144,256]{2,1,0:T(8,128)(2,1)S(1)}, u32[]{:S(2)}, u32[]{:S(2)}) collective-permute-start(bf16[4,144,256]{2,1,0:T(8,128)(2,1)S(1)} %get-tuple-element.51), channel_id=1, source_target_pairs={{0,2},{2,0},{4,6},{6,4},{8,10},{10,8},{12,14},{14,12},{16,18},{18,... | collective-permute-start | bytes 884744 | tf_op jit(solution)/shard_map/ppermute | solution.py:27
  47.7 28.0 %copy-start.10 = (bf16[4,4,144,256]{3,2,1,0:T(8,128)(2,1)}, bf16[4,4,144,256]{3,2,1,0:T(8,128)(2,1)S(1)}, u32[]{:S(2)}) copy-start(bf16[4,4,144,256]{3,2,1,0:T(8,128)(2,1)S(1)} %pad_maximum_fusion.refs_0_) | copy-start | bytes 3538948
  47.7 28.0 %collective-permute-start.17 = (bf16[4,4,144,256]{3,2,1,0:T(8,128)(2,1)S(1)}, bf16[4,4,144,256]{3,2,1,0:T(8,128)(2,1)S(1)}, u32[]{:S(2)}, u32[]{:S(2)}) collective-permute-start(bf16[4,4,144,256]{3,2,1,0:T(8,128)(2,1)S(1)} %pad_maximum_fusion.refs_0_), channel_id=1, source_target_pairs={{0,1},{1,0},{2,3},{3,2},{4,5},{5,4},{6,7},{7,6},{8,9},{9,8},{10,11... | collective-permute-start | bytes 3538952 | tf_op jit(solution)/shard_map/ppermute | solution.py:32
  50.4 9.2 %collective-permute-start.31 = (bf16[256,512]{1,0:T(8,128)(2,1)S(1)}, bf16[256,512]{1,0:T(8,128)(2,1)S(1)}, u32[]{:S(2)}, u32[]{:S(2)}) collective-permute-start(bf16[256,512]{1,0:T(8,128)(2,1)S(1)} %get-tuple-element.43), channel_id=1, source_target_pairs={{0,2},{2,0},{4,6},{6,4},{8,10},{10,8},{12,14},{14,12},{16,18},{18,... | collective-permute-start | bytes 786440 | tf_op jit(solution)/shard_map/ppermute | solution.py:27
  51.9 13.7 %collective-permute-start.32 = (bf16[256,512]{1,0:T(8,128)(2,1)S(1)}, bf16[256,512]{1,0:T(8,128)(2,1)S(1)}, u32[]{:S(2)}, u32[]{:S(2)}) collective-permute-start(bf16[256,512]{1,0:T(8,128)(2,1)S(1)} %get-tuple-element.42), channel_id=1, source_target_pairs={{0,4},{2,6},{4,0},{6,2},{8,12},{10,14},{12,8},{14,10},{16,20},{18,... | collective-permute-start | bytes 786440 | tf_op jit(solution)/shard_map/ppermute | solution.py:27
  52.6 13.0 %collective-permute-start.33 = (bf16[256,512]{1,0:T(8,128)(2,1)S(1)}, bf16[256,512]{1,0:T(8,128)(2,1)S(1)}, u32[]{:S(2)}, u32[]{:S(2)}) collective-permute-start(bf16[256,512]{1,0:T(8,128)(2,1)S(1)} %get-tuple-element.41), channel_id=1, source_target_pairs={{0,6},{2,4},{4,2},{6,0},{8,14},{10,12},{12,10},{14,8},{16,22},{18,... | collective-permute-start | bytes 786440 | tf_op jit(solution)/shard_map/ppermute | solution.py:27
  65.6 2.0 copy-start.1
  67.6 9.1 %copy-start.2 = (bf16[7,512,512]{2,1,0:T(8,128)(2,1)S(1)}, bf16[7,512,512]{2,1,0:T(8,128)(2,1)}, u32[]{:S(2)}) copy-start(bf16[7,512,512]{2,1,0:T(8,128)(2,1)} %refs_8_.5) | copy-start | bytes 11010052
  71.2 13.8 %collective-permute-start.34 = (bf16[4,128,256]{2,1,0:T(8,128)(2,1)S(1)}, bf16[4,128,256]{2,1,0:T(8,128)(2,1)S(1)}, u32[]{:S(2)}, u32[]{:S(2)}) collective-permute-start(bf16[4,128,256]{2,1,0:T(8,128)(2,1)S(1)} %get-tuple-element.40), channel_id=1, source_target_pairs={{0,8},{2,10},{4,12},{6,14},{8,0},{10,2},{12,4},{14,6},{16,24},{18,... | collective-permute-start | bytes 786440 | tf_op jit(solution)/shard_map/ppermute | solution.py:27
  71.8 21.3 %collective-permute-start.35 = (bf16[4,128,256]{2,1,0:T(8,128)(2,1)S(1)}, bf16[4,128,256]{2,1,0:T(8,128)(2,1)S(1)}, u32[]{:S(2)}, u32[]{:S(2)}) collective-permute-start(bf16[4,128,256]{2,1,0:T(8,128)(2,1)S(1)} %get-tuple-element.39.refs_0_), channel_id=1, source_target_pairs={{0,16},{2,18},{4,20},{6,22},{8,24},{10,26},{12,28},{14,30},{16,0},... | collective-permute-start | bytes 786440 | tf_op jit(solution)/shard_map/ppermute | solution.py:27
  74.3 18.8 %collective-permute-start.36 = (bf16[4,128,256]{2,1,0:T(8,128)(2,1)S(1)}, bf16[4,128,256]{2,1,0:T(8,128)(2,1)S(1)}, u32[]{:S(2)}, u32[]{:S(2)}) collective-permute-start(bf16[4,128,256]{2,1,0:T(8,128)(2,1)S(1)} %get-tuple-element.40), channel_id=1, source_target_pairs={{0,24},{2,26},{4,28},{6,30},{8,16},{10,18},{12,20},{14,22},{16,8},... | collective-permute-start | bytes 786440 | tf_op jit(solution)/shard_map/ppermute | solution.py:27
  75.7 1.1 copy-start.15
  76.7 1.3 copy-start.11
  78.0 1.3 copy-start.16
  99.1 1.2 copy-start.7
  100.3 95.9 %all-to-all-start.1 = ((bf16[8,224,256]{2,1,0:T(8,128)(2,1)}), bf16[8,224,256]{2,1,0:T(8,128)(2,1)}, u32[]{:S(2)}, u32[]{:S(2)}) async-start(bf16[8,224,256]{2,1,0:T(8,128)(2,1)} %level12.5), calls=%async_computation.1 | async-start | bytes 1835008 | tf_op jit(solution)/shard_map/all_to_all | solution.py:519
  106.5 33.8 %copy-start.13 = (bf16[512,512]{1,0:T(8,128)(2,1)S(1)}, bf16[512,512]{1,0:T(8,128)(2,1)}, u32[]{:S(2)}) copy-start(bf16[512,512]{1,0:T(8,128)(2,1)} %copy-done.12) | copy-start | bytes 1572868
  108.1 22.2 %collective-permute-start.25 = (bf16[256,1024]{1,0:T(8,128)(2,1)S(1)}, bf16[256,1024]{1,0:T(8,128)(2,1)S(1)}, u32[]{:S(2)}, u32[]{:S(2)}) collective-permute-start(bf16[256,1024]{1,0:T(8,128)(2,1)S(1)} %get-tuple-element.49), channel_id=1, source_target_pairs={{0,2},{2,0},{4,6},{6,4},{8,10},{10,8},{12,14},{14,12},{16,18},{18,... | collective-permute-start | bytes 1572872 | tf_op jit(solution)/shard_map/ppermute | solution.py:27
  110.2 20.9 %collective-permute-start.26 = (bf16[256,1024]{1,0:T(8,128)(2,1)S(1)}, bf16[256,1024]{1,0:T(8,128)(2,1)S(1)}, u32[]{:S(2)}, u32[]{:S(2)}) collective-permute-start(bf16[256,1024]{1,0:T(8,128)(2,1)S(1)} %get-tuple-element.48), channel_id=1, source_target_pairs={{0,4},{2,6},{4,0},{6,2},{8,12},{10,14},{12,8},{14,10},{16,20},{18,... | collective-permute-start | bytes 1572872 | tf_op jit(solution)/shard_map/ppermute | solution.py:27
  111.6 28.7 %collective-permute-start.27 = (bf16[256,1024]{1,0:T(8,128)(2,1)S(1)}, bf16[256,1024]{1,0:T(8,128)(2,1)S(1)}, u32[]{:S(2)}, u32[]{:S(2)}) collective-permute-start(bf16[256,1024]{1,0:T(8,128)(2,1)S(1)} %get-tuple-element.47), channel_id=1, source_target_pairs={{0,6},{2,4},{4,2},{6,0},{8,14},{10,12},{12,10},{14,8},{16,22},{18,... | collective-permute-start | bytes 1572872 | tf_op jit(solution)/shard_map/ppermute | solution.py:27
  140.3 2.0 copy-start.3
  142.4 45.5 %copy-start.4 = (bf16[7,512,512]{2,1,0:T(8,128)(2,1)S(1)}, bf16[7,512,512]{2,1,0:T(8,128)(2,1)}, u32[]{:S(2)}) copy-start(bf16[7,512,512]{2,1,0:T(8,128)(2,1)} %refs_8_.5) | copy-start | bytes 11010052
  142.4 45.5 %copy-start.8 = (bf16[1792,512]{1,0:T(8,128)(2,1)S(1)}, bf16[1792,512]{1,0:T(8,128)(2,1)}, u32[]{:S(2)}) copy-start(bf16[1792,512]{1,0:T(8,128)(2,1)} %copy-done.7) | copy-start | bytes 5505028
  148.0 22.1 %collective-permute-start.28 = (bf16[4,128,512]{2,1,0:T(8,128)(2,1)S(1)}, bf16[4,128,512]{2,1,0:T(8,128)(2,1)S(1)}, u32[]{:S(2)}, u32[]{:S(2)}) collective-permute-start(bf16[4,128,512]{2,1,0:T(8,128)(2,1)S(1)} %get-tuple-element.38), channel_id=1, source_target_pairs={{0,8},{2,10},{4,12},{6,14},{8,0},{10,2},{12,4},{14,6},{16,24},{18,... | collective-permute-start | bytes 1572872 | tf_op jit(solution)/shard_map/ppermute | solution.py:27
  149.5 38.4 %collective-permute-start.29 = (bf16[4,128,512]{2,1,0:T(8,128)(2,1)S(1)}, bf16[4,128,512]{2,1,0:T(8,128)(2,1)S(1)}, u32[]{:S(2)}, u32[]{:S(2)}) collective-permute-start(bf16[4,128,512]{2,1,0:T(8,128)(2,1)S(1)} %get-tuple-element.37.refs_0_), channel_id=1, source_target_pairs={{0,16},{2,18},{4,20},{6,22},{8,24},{10,26},{12,28},{14,30},{16,0},... | collective-permute-start | bytes 1572872 | tf_op jit(solution)/shard_map/ppermute | solution.py:27
  152.7 35.2 %collective-permute-start.30 = (bf16[4,128,512]{2,1,0:T(8,128)(2,1)S(1)}, bf16[4,128,512]{2,1,0:T(8,128)(2,1)S(1)}, u32[]{:S(2)}, u32[]{:S(2)}) collective-permute-start(bf16[4,128,512]{2,1,0:T(8,128)(2,1)S(1)} %get-tuple-element.38), channel_id=1, source_target_pairs={{0,24},{2,26},{4,28},{6,30},{8,16},{10,18},{12,20},{14,22},{16,8},... | collective-permute-start | bytes 1572872 | tf_op jit(solution)/shard_map/ppermute | solution.py:27
  196.2 94.0 %all-to-all-start = ((bf16[8,224,512]{2,1,0:T(8,128)(2,1)}), bf16[8,224,512]{2,1,0:T(8,128)(2,1)}, u32[]{:S(2)}, u32[]{:S(2)}) async-start(bf16[8,224,512]{2,1,0:T(8,128)(2,1)} %level12.4), calls=%async_computation | async-start | bytes 3670016 | tf_op jit(solution)/shard_map/all_to_all | solution.py:519
  207.5 28.8 %collective-permute-start.11 = (bf16[256,512]{1,0:T(8,128)(2,1)}, bf16[256,512]{1,0:T(8,128)(2,1)S(1)}, u32[]{:S(2)}, u32[]{:S(2)}) collective-permute-start(bf16[256,512]{1,0:T(8,128)(2,1)} %get-tuple-element.46), channel_id=1, source_target_pairs={{0,2},{2,0},{4,6},{6,4},{8,10},{10,8},{12,14},{14,12},{16,18},{18,... | collective-permute-start | bytes 786440 | tf_op jit(solution)/shard_map/ppermute | solution.py:27
  209.5 26.8 %collective-permute-start.12 = (bf16[256,512]{1,0:T(8,128)(2,1)}, bf16[256,512]{1,0:T(8,128)(2,1)S(1)}, u32[]{:S(2)}, u32[]{:S(2)}) collective-permute-start(bf16[256,512]{1,0:T(8,128)(2,1)} %get-tuple-element.45), channel_id=1, source_target_pairs={{0,4},{2,6},{4,0},{6,2},{8,12},{10,14},{12,8},{14,10},{16,20},{18,... | collective-permute-start | bytes 786440 | tf_op jit(solution)/shard_map/ppermute | solution.py:27
  210.9 29.5 %collective-permute-start.13 = (bf16[256,512]{1,0:T(8,128)(2,1)S(1)}, bf16[256,512]{1,0:T(8,128)(2,1)S(1)}, u32[]{:S(2)}, u32[]{:S(2)}) collective-permute-start(bf16[256,512]{1,0:T(8,128)(2,1)S(1)} %get-tuple-element.44), channel_id=1, source_target_pairs={{0,6},{2,4},{4,2},{6,0},{8,14},{10,12},{12,10},{14,8},{16,22},{18,... | collective-permute-start | bytes 786440 | tf_op jit(solution)/shard_map/ppermute | solution.py:27
  240.5 2.0 copy-start.5
  242.5 1.0 copy-start.14
  243.6 26.1 %copy-start.6 = (bf16[7,512,512]{2,1,0:T(8,128)(2,1)S(1)}, bf16[7,512,512]{2,1,0:T(8,128)(2,1)}, u32[]{:S(2)}) copy-start(bf16[7,512,512]{2,1,0:T(8,128)(2,1)} %refs_8_.5) | copy-start | bytes 11010052
  243.6 26.1 %copy-start.9 = (bf16[1792,512]{1,0:T(8,128)(2,1)S(1)}, bf16[1792,512]{1,0:T(8,128)(2,1)}, u32[]{:S(2)}) copy-start(bf16[1792,512]{1,0:T(8,128)(2,1)} %copy-done.7) | copy-start | bytes 5505028
  247.1 12.4 %collective-permute-start.14 = (bf16[4,128,256]{2,1,0:T(8,128)(2,1)S(1)}, bf16[4,128,256]{2,1,0:T(8,128)(2,1)S(1)}, u32[]{:S(2)}, u32[]{:S(2)}) collective-permute-start(bf16[4,128,256]{2,1,0:T(8,128)(2,1)S(1)} %get-tuple-element.26), channel_id=1, source_target_pairs={{0,8},{2,10},{4,12},{6,14},{8,0},{10,2},{12,4},{14,6},{16,24},{18,... | collective-permute-start | bytes 786440 | tf_op jit(solution)/shard_map/ppermute | solution.py:27
  248.1 21.5 %collective-permute-start.15 = (bf16[4,128,256]{2,1,0:T(8,128)(2,1)S(1)}, bf16[4,128,256]{2,1,0:T(8,128)(2,1)S(1)}, u32[]{:S(2)}, u32[]{:S(2)}) collective-permute-start(bf16[4,128,256]{2,1,0:T(8,128)(2,1)S(1)} %get-tuple-element.25.refs_0_), channel_id=1, source_target_pairs={{0,16},{2,18},{4,20},{6,22},{8,24},{10,26},{12,28},{14,30},{16,0},... | collective-permute-start | bytes 786440 | tf_op jit(solution)/shard_map/ppermute | solution.py:27
  251.2 18.4 %collective-permute-start.16 = (bf16[4,128,256]{2,1,0:T(8,128)(2,1)S(1)}, bf16[4,128,256]{2,1,0:T(8,128)(2,1)S(1)}, u32[]{:S(2)}, u32[]{:S(2)}) collective-permute-start(bf16[4,128,256]{2,1,0:T(8,128)(2,1)S(1)} %get-tuple-element.26), channel_id=1, source_target_pairs={{0,24},{2,26},{4,28},{6,30},{8,16},{10,18},{12,20},{14,22},{16,8},... | collective-permute-start | bytes 786440 | tf_op jit(solution)/shard_map/ppermute | solution.py:27
  275.4 9.6 %collective-permute-start.18 = (bf16[224,256]{1,0:T(8,128)(2,1)}, bf16[224,256]{1,0:T(8,128)(2,1)S(1)}, u32[]{:S(2)}, u32[]{:S(2)}) collective-permute-start(bf16[224,256]{1,0:T(8,128)(2,1)} %get-tuple-element.30), channel_id=1, source_target_pairs={{0,2},{2,0},{4,6},{6,4},{8,10},{10,8},{12,14},{14,12},{16,18},{18,... | collective-permute-start | bytes 344072 | tf_op jit(solution)/shard_map/ppermute | solution.py:27
  277.7 9.4 %collective-permute-start.19 = (bf16[224,256]{1,0:T(8,128)(2,1)}, bf16[224,256]{1,0:T(8,128)(2,1)S(1)}, u32[]{:S(2)}, u32[]{:S(2)}) collective-permute-start(bf16[224,256]{1,0:T(8,128)(2,1)} %get-tuple-element.31), channel_id=1, source_target_pairs={{0,4},{2,6},{4,0},{6,2},{8,12},{10,14},{12,8},{14,10},{16,20},{18,... | collective-permute-start | bytes 344072 | tf_op jit(solution)/shard_map/ppermute | solution.py:27
  278.3 14.9 %collective-permute-start.20 = (bf16[224,256]{1,0:T(8,128)(2,1)}, bf16[224,256]{1,0:T(8,128)(2,1)S(1)}, u32[]{:S(2)}, u32[]{:S(2)}) collective-permute-start(bf16[224,256]{1,0:T(8,128)(2,1)} %get-tuple-element.32), channel_id=1, source_target_pairs={{0,6},{2,4},{4,2},{6,0},{8,14},{10,12},{12,10},{14,8},{16,22},{18,... | collective-permute-start | bytes 344072 | tf_op jit(solution)/shard_map/ppermute | solution.py:27
  279.2 14.0 %collective-permute-start.21 = (bf16[224,256]{1,0:T(8,128)(2,1)}, bf16[224,256]{1,0:T(8,128)(2,1)S(1)}, u32[]{:S(2)}, u32[]{:S(2)}) collective-permute-start(bf16[224,256]{1,0:T(8,128)(2,1)} %get-tuple-element.33), channel_id=1, source_target_pairs={{0,8},{2,10},{4,12},{6,14},{8,0},{10,2},{12,4},{14,6},{16,24},{18,... | collective-permute-start | bytes 344072 | tf_op jit(solution)/shard_map/ppermute | solution.py:27
  283.6 9.6 %collective-permute-start.22 = (bf16[224,256]{1,0:T(8,128)(2,1)}, bf16[224,256]{1,0:T(8,128)(2,1)S(1)}, u32[]{:S(2)}, u32[]{:S(2)}) collective-permute-start(bf16[224,256]{1,0:T(8,128)(2,1)} %get-tuple-element.34), channel_id=1, source_target_pairs={{0,10},{2,8},{4,14},{6,12},{8,2},{10,0},{12,6},{14,4},{16,26},{18,... | collective-permute-start | bytes 344072 | tf_op jit(solution)/shard_map/ppermute | solution.py:27
  285.0 8.3 %collective-permute-start.23 = (bf16[224,256]{1,0:T(8,128)(2,1)}, bf16[224,256]{1,0:T(8,128)(2,1)S(1)}, u32[]{:S(2)}, u32[]{:S(2)}) collective-permute-start(bf16[224,256]{1,0:T(8,128)(2,1)} %get-tuple-element.35), channel_id=1, source_target_pairs={{0,12},{2,14},{4,8},{6,10},{8,4},{10,6},{12,0},{14,2},{16,28},{18,... | collective-permute-start | bytes 344072 | tf_op jit(solution)/shard_map/ppermute | solution.py:27
  287.1 6.8 %collective-permute-start.24 = (bf16[224,256]{1,0:T(8,128)(2,1)}, bf16[224,256]{1,0:T(8,128)(2,1)S(1)}, u32[]{:S(2)}, u32[]{:S(2)}) collective-permute-start(bf16[224,256]{1,0:T(8,128)(2,1)} %get-tuple-element.36), channel_id=1, source_target_pairs={{0,14},{2,12},{4,10},{6,8},{8,6},{10,4},{12,2},{14,0},{16,30},{18,... | collective-permute-start | bytes 344072 | tf_op jit(solution)/shard_map/ppermute | solution.py:27
  290.2 3.7 %copy-start.17 = (bf16[224,256]{1,0:T(8,128)(2,1)S(1)}, bf16[224,256]{1,0:T(8,128)(2,1)}, u32[]{:S(2)}) copy-start(bf16[224,256]{1,0:T(8,128)(2,1)} %get-tuple-element.29.refs_0_) | copy-start | bytes 344068
where the time goes:
time: 296 us
  waiting for transfers between devices  158 us (53%)
  starting transfers between devices  69.2 us (23%)
  Pallas kernels  46.7 us (16%)
  local copies, waits for them, and re-layouts  19.3 us (7%)
    ppermute x34, waiting for transfers between devices, xor_leaf(): return lax.ppermute(block, 'leaf', [(i, i ^ mask) for i in range(count)])  156 us
    ppermute x34, starting transfers between devices, xor_leaf(): return lax.ppermute(block, 'leaf', [(i, i ^ mask) for i in range(count)])  49.2 us
    pallas_call x3, Pallas kernels, level12(): pl.pallas_call(functools.partial(level12_kernel, share0, share1, share2,...  20 us
    all_to_all x2, starting transfers between devices, on_device(): lax.all_to_all(done[0], 'leaf', 0, 0, axis_index_groups=pairs, tiled=True)  17.5 us
    unnamed x36, local copies, waits for them, and re-layouts  14 us
    pallas_call x3, Pallas kernels, level0(): pl.pallas_call(functools.partial(level0_kernel, share0), out_shape=[jax.S...  12.7 us
    pallas_call x3, Pallas kernels, place(): pl.pallas_call(functools.partial(place_kernel, keep, 2 * group, column),...  6.89 us
  transfers between devices with their start and end apart: 39, of which 21 were waited for; matrix products, arithmetic and copies ran while one was open for 2% of the time, Pallas kernels for 13%

commit v1 on v0

--- a/solution.py
+++ b/solution.py
@@ -13,8 +13,8 @@
 BLOCK = 128
 MAP_ROWS = 16
 MAP_COLS = 12
-SHARES = (1, 2, 1)
-APART = (2,)
+SHARES = (1, 1, 1, 1)
+APART = (1, 2,)
 TILE = 256
 FINAL_TILE = 512
 
@@ -203,10 +203,9 @@
 
 def level12_kernel(gone, share, final, keep, meta, maps, *refs):
     planes = refs[:4]
-    left1_in, left2_in = refs[4:6]
-    inverses = refs[6:9]
-    outs = refs[9:-9]
-    front, parent, nextf, upper, pivots, finals, left1, left2, sems = refs[-9:]
+    left1_in, left2_in, inverse_in = refs[4:7]
+    outs = refs[7:-10]
+    front, parent, nextf, upper, pivots, finals, left1, left2, inverses, sems = refs[-10:]
     group = planes[0].shape[0]
     slabs = 4 * group
     tile = planes[0].shape[2]
@@ -214,13 +213,21 @@
     rest = rows - share
     last = rows - keep
 
+    high = (meta[0] // group) >> 1
+    loads = [
+        pltpu.make_async_copy(inverse_in.at[index], inverses.at[i], sems.at[2 + i])
+        for i, index in enumerate((4 + high, 5 - high, 6))
+    ]
     load1 = pltpu.make_async_copy(left1_in, left1, sems.at[0])
     load2 = pltpu.make_async_copy(left2_in, left2, sems.at[1])
     opening = pl.program_id(0) == 0
 
     @pl.when(opening)
     def _():
+        loads[0].start()
+        loads[1].start()
         load1.start()
+        loads[2].start()
         load2.start()
         front[:, 0:gone, :] = jnp.zeros((slabs, gone, tile), BF16)
         nextf[:, 0:share, :] = jnp.zeros((slabs, share, tile), BF16)
@@ -239,9 +246,11 @@
         return carry
 
     lax.fori_loop(0, slabs, extend1, 0)
-    pl.when(opening)(load1.wait)
     for half in range(2):
-        upper[...] = dot(inverses[half][0], pivots[half]).astype(BF16)
+        pl.when(opening)(loads[half].wait)
+        upper[...] = dot(inverses[half], pivots[half]).astype(BF16)
+        if half == 0:
+            pl.when(opening)(load1.wait)
 
         def reduce1(quad, carry):
             first = half * 2 * group + 4 * quad
@@ -272,7 +281,8 @@
             at = pl.multiple_of(maps[slab, cross_at(2, 0)] * BLOCK, BLOCK)
             taken = own + nextf[slab - 2 * group, pl.ds(at, head), :]
         finals[turn(slab, meta, slabs, final), :] = taken.astype(finals.dtype)[:final]
-    upper[...] = dot(inverses[2][0], finals[...].astype(BF16)).astype(BF16)
+    pl.when(opening)(loads[2].wait)
+    upper[...] = dot(inverses[2], finals[...].astype(BF16)).astype(BF16)
     pl.when(opening)(load2.wait)
     for slab in range(2 * group):
         product = dot(left2[slab * last:(slab + 1) * last, :], upper[...])
@@ -323,6 +333,7 @@
     sizes = chunk_sizes(span)
     starts = [sum(sizes[:k]) for k in range(len(sizes))]
     meta = jnp.stack([leaf, panel]).astype(jnp.int32)
+    inverse_hbm = pltpu.with_memory_space_constraint(pivot_inverse, pltpu.HBM)
     child_columns = pltpu.with_memory_space_constraint(child_front, pltpu.HBM)
     plane_bits = group.bit_length() - 1
 
@@ -372,7 +383,7 @@
         ),
         compiler_params=room((group, rows, PANEL), (group * rest0, PANEL), *[(PANEL, PANEL)] * 4),
         name="lead0",
-    )(meta, near_maps, *near, pivot_inverse)
+    )(meta, near_maps, *near, inverse_hbm)
 
     piece = lax.dynamic_slice(seed, (0, panel * width), (rest0, width))
     piece = jnp.concatenate([piece, map_rows[:, :width]], axis=0)
@@ -443,7 +454,7 @@
                 (7 * group * rows, tile), (2 * group * rest0, PANEL), *[(PANEL, PANEL)] * 2, (PANEL, 4 * tile)
             ),
             name="level0",
-        )(meta, near_maps, child_columns, *received[k], left0, pivot_inverse)
+        )(meta, near_maps, child_columns, *received[k], left0, inverse_hbm)
 
     def level12(planes, apart):
         side = planes[0].shape[2]
@@ -456,8 +467,7 @@
                 grid=(side // tile,),
                 in_specs=[pl.BlockSpec((group, rest0, tile), lambda j, meta, maps: (0, 0, j))] * 4
                 + [anywhere()] * 2
-                + level1_inverses
-                + [inverse_of(lambda p: 6)],
+                + [pl.BlockSpec(memory_space=pltpu.HBM)],
                 out_specs=[pl.BlockSpec((last, tile), lambda j, meta, maps: (0, j))] * (2 * group)
                 if apart
                 else [pl.BlockSpec((2 * group, last, tile), lambda j, meta, maps: (0, 0, j))],
@@ -470,17 +480,18 @@
                     pltpu.VMEM((PANEL, tile), BF16 if share2 % 16 == 0 else F32),
                     pltpu.VMEM((leaf_count * rest1, PANEL), BF16),
                     pltpu.VMEM((2 * group * last, PANEL), BF16),
-                    pltpu.SemaphoreType.DMA((2,)),
+                    pltpu.VMEM((3, PANEL, PANEL), BF16),
+                    pltpu.SemaphoreType.DMA((5,)),
                 ],
             ),
             compiler_params=room(
                 (3 * leaf_count * rows + 8 * group * rest0 + 4 * group * last, tile),
                 (leaf_count * rest1 + 2 * group * last, PANEL),
-                *[(PANEL, PANEL)] * 6,
-                (16 * PANEL, tile),
+                *[(PANEL, PANEL)] * 3,
+                (12 * PANEL, tile),
             ),
             name="level12",
-        )(meta, all_maps, *planes, left1, left2, *[pivot_inverse] * 3)
+        )(meta, all_maps, *planes, left1, left2, pivot_inverse)
 
     def place(k, pieces, slab):
         side = sizes[k] // 2

time: 296 us -> 280 us (0.946)
  waiting for transfers between devices: 158 us -> 135 us
  Pallas kernels: 46.7 us -> 54.9 us
  local copies, waits for them, and re-layouts: 19.3 us -> 11.5 us
  starting transfers between devices: 69.2 us -> 75.4 us
    ppermute x34 -> x47, waiting for transfers between devices: 156 us -> 133 us  [xor_leaf(): return lax.ppermute(block, 'leaf', [(i, i ^ mask) for i in range(count)])]
    ppermute x34 -> x47, starting transfers between devices: 49.2 us -> 58.4 us  [xor_leaf(): return lax.ppermute(block, 'leaf', [(i, i ^ mask) for i in range(count)])]
    unnamed x36 -> x34, local copies, waits for them, and re-layouts: 14 us -> 6.92 us
    pallas_call x3 -> x4, Pallas kernels: 20 us -> 24.1 us  [level12(): pl.pallas_call(functools.partial(level12_kernel, share0, share1, share2,...]
    all_to_all x2, starting transfers between devices: 17.5 us -> 14.5 us  [on_device(): lax.all_to_all(done[0], 'leaf', 0, 0, axis_index_groups=pairs, tiled=True)]
    pallas_call x3 -> x4, Pallas kernels: 12.7 us -> 14.8 us  [level0(): pl.pallas_call(functools.partial(level0_kernel, share0), out_shape=[jax.S...]
    pallas_call x3 -> x4, Pallas kernels: 6.89 us -> 7.87 us  [place(): pl.pallas_call(functools.partial(place_kernel, keep, 2 * group, column),...]
  transfers between devices with their start and end apart: 39 -> 52, of which waited for: 21 -> 26; matrix products, arithmetic and copies ran while one was open for 2% -> 2% of each run, Pallas kernels for 13% -> 16%
where the time goes in v1:
time: 280 us
  waiting for transfers between devices  135 us (48%)
  starting transfers between devices  75.4 us (27%)
  Pallas kernels  54.9 us (20%)
  local copies, waits for them, and re-layouts  11.5 us (4%)
    ppermute x47, waiting for transfers between devices, xor_leaf(): return lax.ppermute(block, 'leaf', [(i, i ^ mask) for i in range(count)])  133 us
    ppermute x47, starting transfers between devices, xor_leaf(): return lax.ppermute(block, 'leaf', [(i, i ^ mask) for i in range(count)])  58.4 us
    pallas_call x4, Pallas kernels, level12(): pl.pallas_call(functools.partial(level12_kernel, share0, share1, share2,...  24.1 us
    pallas_call x4, Pallas kernels, level0(): pl.pallas_call(functools.partial(level0_kernel, share0), out_shape=[jax.S...  14.8 us
    all_to_all x2, starting transfers between devices, on_device(): lax.all_to_all(done[0], 'leaf', 0, 0, axis_index_groups=pairs, tiled=True)  14.5 us
    pallas_call x4, Pallas kernels, place(): pl.pallas_call(functools.partial(place_kernel, keep, 2 * group, column),...  7.87 us
    unnamed x34, local copies, waits for them, and re-layouts  6.92 us
    pallas_call x1, Pallas kernels, on_device(): pl.pallas_call(functools.partial(lead_level12_kernel, share0, share1, kee...  5.73 us
  transfers between devices with their start and end apart: 52, of which 26 were waited for; matrix products, arithmetic and copies ran while one was open for 2% of the time, Pallas kernels for 16%

profile of v1, /device:TPU:0, one launch (start us, length us, event | category | flops | bytes accessed | tf_op | source)
XLA Modules:
  0.0 279.7 jit_solution(9469251538020424090)
XLA Ops:
  0.9 2.4 collective-permute-start
  5.3 2.4 collective-permute-start.2
  7.7 1.5 collective-permute-start.1
  9.2 2.6 collective-permute-done.2
  11.8 2.4 collective-permute-done.1
  14.2 1.9 collective-permute-done.3
  16.3 1.9 collective-permute-done.4.refs_1_
  18.2 2.4 lead0.1
  20.7 2.8 %collective-permute-start.6 = (bf16[144,256]{1,0:T(8,128)(2,1)S(1)}, bf16[144,256]{1,0:T(8,128)(2,1)S(1)}, u32[]{:S(2)}, u32[]{:S(2)}) collective-permute-start(bf16[144,256]{1,0:T(8,128)(2,1)S(1)} %get-tuple-element.78), channel_id=1, source_target_pairs={{0,16},{2,18},{4,20},{6,22},{8,24},{10,26},{12,28},{14,30},{16,0},... | collective-permute-start | bytes 221192 | tf_op jit(solution)/shard_map/ppermute | solution.py:27
  23.5 1.6 collective-permute-start.5
  25.1 2.4 collective-permute-done.6
  28.0 3.2 %collective-permute-done.7 = bf16[144,256]{1,0:T(8,128)(2,1)S(1)} collective-permute-done((bf16[144,256]{1,0:T(8,128)(2,1)S(1)}, bf16[144,256]{1,0:T(8,128)(2,1)S(1)}, u32[]{:S(2)}, u32[]{:S(2)}) %collective-permute-start.7) | collective-permute-done | bytes 73760 | tf_op jit(solution)/shard_map/ppermute | solution.py:27
  31.3 1.6 collective-permute-start.9
  32.9 1.5 collective-permute-start.8
  34.8 5.5 %collective-permute-done.9 = bf16[4,144,256]{2,1,0:T(8,128)(2,1)S(1)} collective-permute-done((bf16[4,144,256]{2,1,0:T(8,128)(2,1)S(1)}, bf16[4,144,256]{2,1,0:T(8,128)(2,1)S(1)}, u32[]{:S(2)}, u32[]{:S(2)}) %collective-permute-start.9) | collective-permute-done | bytes 294944 | tf_op jit(solution)/shard_map/ppermute | solution.py:27
  40.3 2.4 collective-permute-done.8
  42.7 3.5 %collective-permute-done.10 = bf16[4,144,256]{2,1,0:T(8,128)(2,1)S(1)} collective-permute-done((bf16[4,144,256]{2,1,0:T(8,128)(2,1)S(1)}, bf16[4,144,256]{2,1,0:T(8,128)(2,1)S(1)}, u32[]{:S(2)}, u32[]{:S(2)}) %collective-permute-start.10) | collective-permute-done | bytes 294944 | tf_op jit(solution)/shard_map/ppermute | solution.py:27
  46.6 3.5 %constant_dynamic-slice_fusion = (bf16[256,512]{1,0:T(8,128)(2,1)S(1)}, bf16[256,512]{1,0:T(8,128)(2,1)S(1)}, bf16[256,512]{1,0:T(8,128)(2,1)S(1)}, bf16[256,512...) fusion(bf16[256,8192]{1,0:T(8,128)(2,1)} %refs_0_.7, ...), kind=kLoop, calls=%fused_computation.8 | loop fusion | bytes 6291504 | tf_op jit(solution)/shard_map/dynamic_slice | solution.py:357
  50.0 2.5 collective-permute-start.46
  53.5 6.6 %collective-permute-done.46.refs_3_ = bf16[256,512]{1,0:T(8,128)(2,1)S(1)} collective-permute-done((bf16[256,512]{1,0:T(8,128)(2,1)S(1)}, bf16[256,512]{1,0:T(8,128)(2,1)S(1)}, u32[]{:S(2)}, u32[]{:S(2)}) %collective-permute-start.46) | collective-permute-done | bytes 262176 | tf_op jit(solution)/shard_map/ppermute | solution.py:27
  60.2 4.8 %collective-permute-done.45.refs_2_ = bf16[256,512]{1,0:T(8,128)(2,1)S(1)} collective-permute-done((bf16[256,512]{1,0:T(8,128)(2,1)S(1)}, bf16[256,512]{1,0:T(8,128)(2,1)S(1)}, u32[]{:S(2)}, u32[]{:S(2)}) %collective-permute-start.45) | collective-permute-done | bytes 262176 | tf_op jit(solution)/shard_map/ppermute | solution.py:27
  65.0 3.8 %level0.7 = (bf16[4,128,256]{2,1,0:T(8,128)(2,1)S(1)}, bf16[4,128,256]{2,1,0:T(8,128)(2,1)S(1)}) custom-call(s32[2]{0:T(128)S(1)} %pad_add_fusion.meta, s32[4,12]{1,0:T(4,128)S(1)} %bitcast.32, bf16[256,8192]{1,0:T(8,128)(2,1)} %refs_0_.7, bf16[256,512]{1,0:T(8,128)(2,1)S(1)} %collective-permute-done.44.refs_1_, ...), custom_call_target="tpu_custom_call" | custom-call | tf_op jit(solution)/shard_map/level0/pallas_call | solution.py:435
  68.8 3.8 %collective-permute-start.48 = (bf16[4,128,256]{2,1,0:T(8,128)(2,1)S(1)}, bf16[4,128,256]{2,1,0:T(8,128)(2,1)S(1)}, u32[]{:S(2)}, u32[]{:S(2)}) collective-permute-start(bf16[4,128,256]{2,1,0:T(8,128)(2,1)S(1)} %get-tuple-element.59.refs_0_), channel_id=1, source_target_pairs={{0,16},{2,18},{4,20},{6,22},{8,24},{10,26},{12,28},{14,30},{16,0},... | collective-permute-start | bytes 786440 | tf_op jit(solution)/shard_map/ppermute | solution.py:27
  74.3 1.3 copy-done.10
  75.6 1.3 copy-done.12
  76.9 5.7 %lead12.1 = (bf16[3072,512]{1,0:T(8,128)(2,1)S(1)}, bf16[1792,512]{1,0:T(8,128)(2,1)S(1)}) custom-call(s32[2]{0:T(128)S(1)} %pad_add_fusion.meta, s32[16,12]{1,0:T(8,128)S(1)} %bitcast.26, bf16[4,4,144,256]{3,2,1,0:T(8,128)(2,1)S(1)} %copy-done.10, bf16[4,4,144,256]{3,2,1,0:T(8,128)(2,1)S(1)} %copy-done.12, bf16[7,512,512]{2,1,0:T(8,128)(2,1)S(1)} %copy-done, ...), custom_call_target="tpu_custom_call" | custom-call | tf_op jit(solution)/shard_map/lead12/pallas_call | solution.py:398
  82.6 7.9 %collective-permute-done.48.refs_2_ = bf16[4,128,256]{2,1,0:T(8,128)(2,1)S(1)} collective-permute-done((bf16[4,128,256]{2,1,0:T(8,128)(2,1)S(1)}, bf16[4,128,256]{2,1,0:T(8,128)(2,1)S(1)}, u32[]{:S(2)}, u32[]{:S(2)}) %collective-permute-start.48) | collective-permute-done | bytes 262176 | tf_op jit(solution)/shard_map/ppermute | solution.py:27
  91.6 6.1 %level12.7 = bf16[8,224,256]{2,1,0:T(8,128)(2,1)} custom-call(s32[2]{0:T(128)S(1)} %pad_add_fusion.meta, s32[16,12]{1,0:T(8,128)S(1)} %bitcast.27, bf16[4,128,256]{2,1,0:T(8,128)(2,1)S(1)} %get-tuple-element.59.refs_0_, bf16[4,128,256]{2,1,0:T(8,128)(2,1)S(1)} %collective-permute-done.47.refs_1_, bf16[4,128,256]{2,1,0:T(8,128)(2,1)S(1)} %collective-permute-done.48.refs_2_, ...), custom_call_target="tpu_custom_call" | custom-call | tf_op jit(solution)/shard_map/level12/pallas_call | solution.py:462
  99.0 7.1 %all-to-all-start.1 = ((bf16[8,224,256]{2,1,0:T(8,128)(2,1)}), bf16[8,224,256]{2,1,0:T(8,128)(2,1)}, u32[]{:S(2)}, u32[]{:S(2)}) async-start(bf16[8,224,256]{2,1,0:T(8,128)(2,1)} %level12.7), calls=%async_computation.1 | async-start | bytes 1835008 | tf_op jit(solution)/shard_map/all_to_all | solution.py:530
  106.1 2.9 %collective-permute-start.13 = (bf16[256,512]{1,0:T(8,128)(2,1)}, bf16[256,512]{1,0:T(8,128)(2,1)S(1)}, u32[]{:S(2)}, u32[]{:S(2)}) collective-permute-start(bf16[256,512]{1,0:T(8,128)(2,1)} %get-tuple-element.70), channel_id=1, source_target_pairs={{0,6},{2,4},{4,2},{6,0},{8,14},{10,12},{12,10},{14,8},{16,22},{18,... | collective-permute-start | bytes 786440 | tf_op jit(solution)/shard_map/ppermute | solution.py:27
  109.6 16.5 %collective-permute-done.13.refs_3_ = bf16[256,512]{1,0:T(8,128)(2,1)S(1)} collective-permute-done((bf16[256,512]{1,0:T(8,128)(2,1)}, bf16[256,512]{1,0:T(8,128)(2,1)S(1)}, u32[]{:S(2)}, u32[]{:S(2)}) %collective-permute-start.13) | collective-permute-done | bytes 262176 | tf_op jit(solution)/shard_map/ppermute | solution.py:27
  126.1 3.6 %collective-permute-done.12.refs_2_ = bf16[256,512]{1,0:T(8,128)(2,1)S(1)} collective-permute-done((bf16[256,512]{1,0:T(8,128)(2,1)}, bf16[256,512]{1,0:T(8,128)(2,1)S(1)}, u32[]{:S(2)}, u32[]{:S(2)}) %collective-permute-start.12) | collective-permute-done | bytes 262176 | tf_op jit(solution)/shard_map/ppermute | solution.py:27
  130.8 3.8 %level0.4 = (bf16[4,128,256]{2,1,0:T(8,128)(2,1)S(1)}, bf16[4,128,256]{2,1,0:T(8,128)(2,1)S(1)}) custom-call(s32[2]{0:T(128)S(1)} %pad_add_fusion.meta, s32[4,12]{1,0:T(4,128)S(1)} %bitcast.33, bf16[256,8192]{1,0:T(8,128)(2,1)} %refs_0_.7, bf16[256,512]{1,0:T(8,128)(2,1)S(1)} %collective-permute-done.11.refs_1_, ...), custom_call_target="tpu_custom_call" | custom-call | tf_op jit(solution)/shard_map/level0/pallas_call | solution.py:435
  134.5 1.5 collective-permute-start.15
  136.0 2.7 collective-permute-start.16
  138.8 17.0 %collective-permute-done.15.refs_2_ = bf16[4,128,256]{2,1,0:T(8,128)(2,1)S(1)} collective-permute-done((bf16[4,128,256]{2,1,0:T(8,128)(2,1)S(1)}, bf16[4,128,256]{2,1,0:T(8,128)(2,1)S(1)}, u32[]{:S(2)}, u32[]{:S(2)}) %collective-permute-start.15) | collective-permute-done | bytes 262176 | tf_op jit(solution)/shard_map/ppermute | solution.py:27
  155.8 6.2 %level12.4 = bf16[8,224,256]{2,1,0:T(8,128)(2,1)} custom-call(s32[2]{0:T(128)S(1)} %pad_add_fusion.meta, s32[16,12]{1,0:T(8,128)S(1)} %bitcast.28, bf16[4,128,256]{2,1,0:T(8,128)(2,1)S(1)} %get-tuple-element.35.refs_0_, bf16[4,128,256]{2,1,0:T(8,128)(2,1)S(1)} %collective-permute-done.14.refs_1_, bf16[4,128,256]{2,1,0:T(8,128)(2,1)S(1)} %collective-permute-done.15.refs_2_, ...), custom_call_target="tpu_custom_call" | custom-call | tf_op jit(solution)/shard_map/level12/pallas_call | solution.py:462
  162.0 7.4 %all-to-all-start = ((bf16[8,224,256]{2,1,0:T(8,128)(2,1)}), bf16[8,224,256]{2,1,0:T(8,128)(2,1)}, u32[]{:S(2)}, u32[]{:S(2)}) async-start(bf16[8,224,256]{2,1,0:T(8,128)(2,1)} %level12.4), calls=%async_computation | async-start | bytes 1835008 | tf_op jit(solution)/shard_map/all_to_all | solution.py:530
  169.4 2.9 %collective-permute-start.33 = (bf16[256,512]{1,0:T(8,128)(2,1)}, bf16[256,512]{1,0:T(8,128)(2,1)S(1)}, u32[]{:S(2)}, u32[]{:S(2)}) collective-permute-start(bf16[256,512]{1,0:T(8,128)(2,1)} %get-tuple-element.64), channel_id=1, source_target_pairs={{0,6},{2,4},{4,2},{6,0},{8,14},{10,12},{12,10},{14,8},{16,22},{18,... | collective-permute-start | bytes 786440 | tf_op jit(solution)/shard_map/ppermute | solution.py:27
  172.9 2.9 %collective-permute-start.20 = (bf16[256,512]{1,0:T(8,128)(2,1)}, bf16[256,512]{1,0:T(8,128)(2,1)S(1)}, u32[]{:S(2)}, u32[]{:S(2)}) collective-permute-start(bf16[256,512]{1,0:T(8,128)(2,1)} %get-tuple-element.67), channel_id=1, source_target_pairs={{0,6},{2,4},{4,2},{6,0},{8,14},{10,12},{12,10},{14,8},{16,22},{18,... | collective-permute-start | bytes 786440 | tf_op jit(solution)/shard_map/ppermute | solution.py:27
  176.3 12.1 %collective-permute-done.33.refs_3_ = bf16[256,512]{1,0:T(8,128)(2,1)S(1)} collective-permute-done((bf16[256,512]{1,0:T(8,128)(2,1)}, bf16[256,512]{1,0:T(8,128)(2,1)S(1)}, u32[]{:S(2)}, u32[]{:S(2)}) %collective-permute-start.33) | collective-permute-done | bytes 262176 | tf_op jit(solution)/shard_map/ppermute | solution.py:27
  189.1 10.6 %collective-permute-done.32.refs_2_ = bf16[256,512]{1,0:T(8,128)(2,1)S(1)} collective-permute-done((bf16[256,512]{1,0:T(8,128)(2,1)}, bf16[256,512]{1,0:T(8,128)(2,1)S(1)}, u32[]{:S(2)}, u32[]{:S(2)}) %collective-permute-start.32) | collective-permute-done | bytes 262176 | tf_op jit(solution)/shard_map/ppermute | solution.py:27
  200.7 3.5 %level0.6 = (bf16[4,128,256]{2,1,0:T(8,128)(2,1)S(1)}, bf16[4,128,256]{2,1,0:T(8,128)(2,1)S(1)}) custom-call(s32[2]{0:T(128)S(1)} %pad_add_fusion.meta, s32[4,12]{1,0:T(4,128)S(1)} %bitcast.34, bf16[256,8192]{1,0:T(8,128)(2,1)} %refs_0_.7, bf16[256,512]{1,0:T(8,128)(2,1)S(1)} %collective-permute-done.31.refs_1_, ...), custom_call_target="tpu_custom_call" | custom-call | tf_op jit(solution)/shard_map/level0/pallas_call | solution.py:435
  204.3 2.2 collective-permute-start.36
  206.5 1.3 collective-permute-start.34
  207.8 3.8 %level0.5 = (bf16[4,128,256]{2,1,0:T(8,128)(2,1)S(1)}, bf16[4,128,256]{2,1,0:T(8,128)(2,1)S(1)}) custom-call(s32[2]{0:T(128)S(1)} %pad_add_fusion.meta, s32[4,12]{1,0:T(4,128)S(1)} %bitcast.35, bf16[256,8192]{1,0:T(8,128)(2,1)} %refs_0_.7, bf16[256,512]{1,0:T(8,128)(2,1)S(1)} %collective-permute-done.18.refs_1_, ...), custom_call_target="tpu_custom_call" | custom-call | tf_op jit(solution)/shard_map/level0/pallas_call | solution.py:435
  212.6 2.1 collective-permute-start.23
  214.8 11.8 %collective-permute-done.35.refs_2_ = bf16[4,128,256]{2,1,0:T(8,128)(2,1)S(1)} collective-permute-done((bf16[4,128,256]{2,1,0:T(8,128)(2,1)S(1)}, bf16[4,128,256]{2,1,0:T(8,128)(2,1)S(1)}, u32[]{:S(2)}, u32[]{:S(2)}) %collective-permute-start.35) | collective-permute-done | bytes 262176 | tf_op jit(solution)/shard_map/ppermute | solution.py:27
  226.6 5.9 %level12.6 = (bf16[224,256]{1,0:T(8,128)(2,1)}, bf16[224,256]{1,0:T(8,128)(2,1)}, bf16[224,256]{1,0:T(8,128)(2,1)}, bf16[224,256]{1,0:T(8,128)(2,1)}, bf16[224,2...) custom-call(s32[2]{0:T(128)S(1)} %pad_add_fusion.meta, ...), custom_call_target="tpu_custom_call" | custom-call | tf_op jit(solution)/shard_map/level12/pallas_call | solution.py:462
  232.7 9.4 %collective-permute-done.22.refs_2_ = bf16[4,128,256]{2,1,0:T(8,128)(2,1)S(1)} collective-permute-done((bf16[4,128,256]{2,1,0:T(8,128)(2,1)S(1)}, bf16[4,128,256]{2,1,0:T(8,128)(2,1)S(1)}, u32[]{:S(2)}, u32[]{:S(2)}) %collective-permute-start.22) | collective-permute-done | bytes 262176 | tf_op jit(solution)/shard_map/ppermute | solution.py:27
  243.0 3.5 %collective-permute-start.40 = (bf16[224,256]{1,0:T(8,128)(2,1)}, bf16[224,256]{1,0:T(8,128)(2,1)S(1)}, u32[]{:S(2)}, u32[]{:S(2)}) collective-permute-start(bf16[224,256]{1,0:T(8,128)(2,1)} %get-tuple-element.55), channel_id=1, source_target_pairs={{0,8},{2,10},{4,12},{6,14},{8,0},{10,2},{12,4},{14,6},{16,24},{18,... | collective-permute-start | bytes 344072 | tf_op jit(solution)/shard_map/ppermute | solution.py:27
  247.7 5.9 %level12.5 = (bf16[224,256]{1,0:T(8,128)(2,1)}, bf16[224,256]{1,0:T(8,128)(2,1)}, bf16[224,256]{1,0:T(8,128)(2,1)}, bf16[224,256]{1,0:T(8,128)(2,1)}, bf16[224,2...) custom-call(s32[2]{0:T(128)S(1)} %pad_add_fusion.meta, ...), custom_call_target="tpu_custom_call" | custom-call | tf_op jit(solution)/shard_map/level12/pallas_call | solution.py:462
  253.6 2.2 collective-permute-start.42
  256.5 1.5 collective-permute-start.24
  258.8 1.3 collective-permute-start.26
  261.1 1.2 collective-permute-start.27
  262.6 1.8 collective-permute-start.28
  264.3 1.3 collective-permute-start.29
  265.7 2.9 %collective-permute-done.25.refs_2_ = bf16[224,256]{1,0:T(8,128)(2,1)S(1)} collective-permute-done((bf16[224,256]{1,0:T(8,128)(2,1)}, bf16[224,256]{1,0:T(8,128)(2,1)S(1)}, u32[]{:S(2)}, u32[]{:S(2)}) %collective-permute-start.25) | collective-permute-done | bytes 114720 | tf_op jit(solution)/shard_map/ppermute | solution.py:27
  268.6 2.3 place.4.refs_8_
  270.9 1.6 place.5.refs_8_
  272.6 3.0 %collective-permute-done.30.refs_7_ = bf16[224,256]{1,0:T(8,128)(2,1)S(1)} collective-permute-done((bf16[224,256]{1,0:T(8,128)(2,1)}, bf16[224,256]{1,0:T(8,128)(2,1)S(1)}, u32[]{:S(2)}, u32[]{:S(2)}) %collective-permute-start.30) | collective-permute-done | bytes 114720 | tf_op jit(solution)/shard_map/ppermute | solution.py:27
  275.6 1.6 place.6.refs_1_
  277.3 2.3 place.7
  (106 shorter events, 20.2 us)
Async XLA Ops:
  0.9 3.4 %collective-permute-start = (bf16[256,256]{1,0:T(8,128)(2,1)S(1)}, bf16[256,256]{1,0:T(8,128)(2,1)S(1)}, u32[]{:S(2)}, u32[]{:S(2)}) collective-permute-start(bf16[256,256]{1,0:T(8,128)(2,1)S(1)} %slice.16), channel_id=1, source_target_pairs={{0,1},{2,3},{4,5},{6,7},{8,9},{10,11},{12,13},{14,15},{16,17},{18,... | collective-permute-start | bytes 393224 | tf_op jit(solution)/shard_map/ppermute | solution.py:345
  5.3 6.6 %collective-permute-start.2 = (bf16[272,256]{1,0:T(8,128)(2,1)S(1)}, bf16[272,256]{1,0:T(8,128)(2,1)S(1)}, u32[]{:S(2)}, u32[]{:S(2)}) collective-permute-start(bf16[272,256]{1,0:T(8,128)(2,1)S(1)} %get-tuple-element.76), channel_id=1, source_target_pairs={{0,4},{2,6},{4,0},{6,2},{8,12},{10,14},{12,8},{14,10},{16,20},{18,... | collective-permute-start | bytes 417800 | tf_op jit(solution)/shard_map/ppermute | solution.py:27
  7.7 6.5 %collective-permute-start.1 = (bf16[272,256]{1,0:T(8,128)(2,1)S(1)}, bf16[272,256]{1,0:T(8,128)(2,1)S(1)}, u32[]{:S(2)}, u32[]{:S(2)}) collective-permute-start(bf16[272,256]{1,0:T(8,128)(2,1)S(1)} %get-tuple-element.76), channel_id=1, source_target_pairs={{0,2},{2,0},{4,6},{6,4},{8,10},{10,8},{12,14},{14,12},{16,18},{18,... | collective-permute-start | bytes 417800 | tf_op jit(solution)/shard_map/ppermute | solution.py:27
  9.2 6.9 %collective-permute-start.3 = (bf16[272,256]{1,0:T(8,128)(2,1)S(1)}, bf16[272,256]{1,0:T(8,128)(2,1)S(1)}, u32[]{:S(2)}, u32[]{:S(2)}) collective-permute-start(bf16[272,256]{1,0:T(8,128)(2,1)S(1)} %get-tuple-element.76), channel_id=1, source_target_pairs={{0,6},{2,4},{4,2},{6,0},{8,14},{10,12},{12,10},{14,8},{16,22},{18,... | collective-permute-start | bytes 417800 | tf_op jit(solution)/shard_map/ppermute | solution.py:27
  16.2 2.0 collective-permute-start.4
  20.6 44.4 %copy-start.6 = (bf16[512,512]{1,0:T(8,128)(2,1)}, bf16[512,512]{1,0:T(8,128)(2,1)S(1)}, u32[]{:S(2)}) copy-start(bf16[512,512]{1,0:T(8,128)(2,1)S(1)} %get-tuple-element.34.refs_4_) | copy-start | bytes 1572868
  20.7 6.8 %collective-permute-start.6 = (bf16[144,256]{1,0:T(8,128)(2,1)S(1)}, bf16[144,256]{1,0:T(8,128)(2,1)S(1)}, u32[]{:S(2)}, u32[]{:S(2)}) collective-permute-start(bf16[144,256]{1,0:T(8,128)(2,1)S(1)} %get-tuple-element.78), channel_id=1, source_target_pairs={{0,16},{2,18},{4,20},{6,22},{8,24},{10,26},{12,28},{14,30},{16,0},... | collective-permute-start | bytes 221192 | tf_op jit(solution)/shard_map/ppermute | solution.py:27
  23.5 4.5 %collective-permute-start.5 = (bf16[144,256]{1,0:T(8,128)(2,1)S(1)}, bf16[144,256]{1,0:T(8,128)(2,1)S(1)}, u32[]{:S(2)}, u32[]{:S(2)}) collective-permute-start(bf16[144,256]{1,0:T(8,128)(2,1)S(1)} %get-tuple-element.78), channel_id=1, source_target_pairs={{0,8},{2,10},{4,12},{6,14},{8,0},{10,2},{12,4},{14,6},{16,24},{18,... | collective-permute-start | bytes 221192 | tf_op jit(solution)/shard_map/ppermute | solution.py:27
  25.1 6.2 %collective-permute-start.7 = (bf16[144,256]{1,0:T(8,128)(2,1)S(1)}, bf16[144,256]{1,0:T(8,128)(2,1)S(1)}, u32[]{:S(2)}, u32[]{:S(2)}) collective-permute-start(bf16[144,256]{1,0:T(8,128)(2,1)S(1)} %get-tuple-element.78), channel_id=1, source_target_pairs={{0,24},{2,26},{4,28},{6,30},{8,16},{10,18},{12,20},{14,22},{16,8},... | collective-permute-start | bytes 221192 | tf_op jit(solution)/shard_map/ppermute | solution.py:27
  31.3 9.0 %collective-permute-start.9 = (bf16[4,144,256]{2,1,0:T(8,128)(2,1)S(1)}, bf16[4,144,256]{2,1,0:T(8,128)(2,1)S(1)}, u32[]{:S(2)}, u32[]{:S(2)}) collective-permute-start(bf16[4,144,256]{2,1,0:T(8,128)(2,1)S(1)} %get-tuple-element.74), channel_id=1, source_target_pairs={{0,4},{2,6},{4,0},{6,2},{8,12},{10,14},{12,8},{14,10},{16,20},{18,... | collective-permute-start | bytes 884744 | tf_op jit(solution)/shard_map/ppermute | solution.py:27
  32.9 9.9 %collective-permute-start.8 = (bf16[4,144,256]{2,1,0:T(8,128)(2,1)S(1)}, bf16[4,144,256]{2,1,0:T(8,128)(2,1)S(1)}, u32[]{:S(2)}, u32[]{:S(2)}) collective-permute-start(bf16[4,144,256]{2,1,0:T(8,128)(2,1)S(1)} %get-tuple-element.74), channel_id=1, source_target_pairs={{0,2},{2,0},{4,6},{6,4},{8,10},{10,8},{12,14},{14,12},{16,18},{18,... | collective-permute-start | bytes 884744 | tf_op jit(solution)/shard_map/ppermute | solution.py:27
  34.4 11.9 %collective-permute-start.10 = (bf16[4,144,256]{2,1,0:T(8,128)(2,1)S(1)}, bf16[4,144,256]{2,1,0:T(8,128)(2,1)S(1)}, u32[]{:S(2)}, u32[]{:S(2)}) collective-permute-start(bf16[4,144,256]{2,1,0:T(8,128)(2,1)S(1)} %get-tuple-element.74), channel_id=1, source_target_pairs={{0,6},{2,4},{4,2},{6,0},{8,14},{10,12},{12,10},{14,8},{16,22},{18,... | collective-permute-start | bytes 884744 | tf_op jit(solution)/shard_map/ppermute | solution.py:27
  46.4 26.8 %copy-start.9 = (bf16[4,4,144,256]{3,2,1,0:T(8,128)(2,1)}, bf16[4,4,144,256]{3,2,1,0:T(8,128)(2,1)S(1)}, u32[]{:S(2)}) copy-start(bf16[4,4,144,256]{3,2,1,0:T(8,128)(2,1)S(1)} %pad_maximum_fusion.refs_0_) | copy-start | bytes 3538948
  46.5 26.8 %collective-permute-start.17 = (bf16[4,4,144,256]{3,2,1,0:T(8,128)(2,1)S(1)}, bf16[4,4,144,256]{3,2,1,0:T(8,128)(2,1)S(1)}, u32[]{:S(2)}, u32[]{:S(2)}) collective-permute-start(bf16[4,4,144,256]{3,2,1,0:T(8,128)(2,1)S(1)} %pad_maximum_fusion.refs_0_), channel_id=1, source_target_pairs={{0,1},{1,0},{2,3},{3,2},{4,5},{5,4},{6,7},{7,6},{8,9},{9,8},{10,11... | collective-permute-start | bytes 3538952 | tf_op jit(solution)/shard_map/ppermute | solution.py:32
  50.0 10.1 %collective-permute-start.46 = (bf16[256,512]{1,0:T(8,128)(2,1)S(1)}, bf16[256,512]{1,0:T(8,128)(2,1)S(1)}, u32[]{:S(2)}, u32[]{:S(2)}) collective-permute-start(bf16[256,512]{1,0:T(8,128)(2,1)S(1)} %get-tuple-element.61), channel_id=1, source_target_pairs={{0,6},{2,4},{4,2},{6,0},{8,14},{10,12},{12,10},{14,8},{16,22},{18,... | collective-permute-start | bytes 786440 | tf_op jit(solution)/shard_map/ppermute | solution.py:27
  52.5 12.4 %collective-permute-start.45 = (bf16[256,512]{1,0:T(8,128)(2,1)S(1)}, bf16[256,512]{1,0:T(8,128)(2,1)S(1)}, u32[]{:S(2)}, u32[]{:S(2)}) collective-permute-start(bf16[256,512]{1,0:T(8,128)(2,1)S(1)} %get-tuple-element.62), channel_id=1, source_target_pairs={{0,4},{2,6},{4,0},{6,2},{8,12},{10,14},{12,8},{14,10},{16,20},{18,... | collective-permute-start | bytes 786440 | tf_op jit(solution)/shard_map/ppermute | solution.py:27
  53.0 12.0 %collective-permute-start.44 = (bf16[256,512]{1,0:T(8,128)(2,1)S(1)}, bf16[256,512]{1,0:T(8,128)(2,1)S(1)}, u32[]{:S(2)}, u32[]{:S(2)}) collective-permute-start(bf16[256,512]{1,0:T(8,128)(2,1)S(1)} %get-tuple-element.63), channel_id=1, source_target_pairs={{0,2},{2,0},{4,6},{6,4},{8,10},{10,8},{12,14},{14,12},{16,18},{18,... | collective-permute-start | bytes 786440 | tf_op jit(solution)/shard_map/ppermute | solution.py:27
  65.0 9.3 %copy-start = (bf16[7,512,512]{2,1,0:T(8,128)(2,1)S(1)}, bf16[7,512,512]{2,1,0:T(8,128)(2,1)}, u32[]{:S(2)}) copy-start(bf16[7,512,512]{2,1,0:T(8,128)(2,1)} %refs_6_.7) | copy-start | bytes 11010052
  68.8 21.7 %collective-permute-start.48 = (bf16[4,128,256]{2,1,0:T(8,128)(2,1)S(1)}, bf16[4,128,256]{2,1,0:T(8,128)(2,1)S(1)}, u32[]{:S(2)}, u32[]{:S(2)}) collective-permute-start(bf16[4,128,256]{2,1,0:T(8,128)(2,1)S(1)} %get-tuple-element.59.refs_0_), channel_id=1, source_target_pairs={{0,16},{2,18},{4,20},{6,22},{8,24},{10,26},{12,28},{14,30},{16,0},... | collective-permute-start | bytes 786440 | tf_op jit(solution)/shard_map/ppermute | solution.py:27
  72.6 17.9 %collective-permute-start.49 = (bf16[4,128,256]{2,1,0:T(8,128)(2,1)S(1)}, bf16[4,128,256]{2,1,0:T(8,128)(2,1)S(1)}, u32[]{:S(2)}, u32[]{:S(2)}) collective-permute-start(bf16[4,128,256]{2,1,0:T(8,128)(2,1)S(1)} %get-tuple-element.60), channel_id=1, source_target_pairs={{0,24},{2,26},{4,28},{6,30},{8,16},{10,18},{12,20},{14,22},{16,8},... | collective-permute-start | bytes 786440 | tf_op jit(solution)/shard_map/ppermute | solution.py:27
  73.1 18.6 %collective-permute-start.47 = (bf16[4,128,256]{2,1,0:T(8,128)(2,1)S(1)}, bf16[4,128,256]{2,1,0:T(8,128)(2,1)S(1)}, u32[]{:S(2)}, u32[]{:S(2)}) collective-permute-start(bf16[4,128,256]{2,1,0:T(8,128)(2,1)S(1)} %get-tuple-element.60), channel_id=1, source_target_pairs={{0,8},{2,10},{4,12},{6,14},{8,0},{10,2},{12,4},{14,6},{16,24},{18,... | collective-permute-start | bytes 786440 | tf_op jit(solution)/shard_map/ppermute | solution.py:27
  74.3 1.3 copy-start.10
  99.0 63.0 %all-to-all-start.1 = ((bf16[8,224,256]{2,1,0:T(8,128)(2,1)}), bf16[8,224,256]{2,1,0:T(8,128)(2,1)}, u32[]{:S(2)}, u32[]{:S(2)}) async-start(bf16[8,224,256]{2,1,0:T(8,128)(2,1)} %level12.7), calls=%async_computation.1 | async-start | bytes 1835008 | tf_op jit(solution)/shard_map/all_to_all | solution.py:530
  106.1 20.0 %collective-permute-start.13 = (bf16[256,512]{1,0:T(8,128)(2,1)}, bf16[256,512]{1,0:T(8,128)(2,1)S(1)}, u32[]{:S(2)}, u32[]{:S(2)}) collective-permute-start(bf16[256,512]{1,0:T(8,128)(2,1)} %get-tuple-element.70), channel_id=1, source_target_pairs={{0,6},{2,4},{4,2},{6,0},{8,14},{10,12},{12,10},{14,8},{16,22},{18,... | collective-permute-start | bytes 786440 | tf_op jit(solution)/shard_map/ppermute | solution.py:27
  109.0 20.7 %collective-permute-start.12 = (bf16[256,512]{1,0:T(8,128)(2,1)}, bf16[256,512]{1,0:T(8,128)(2,1)S(1)}, u32[]{:S(2)}, u32[]{:S(2)}) collective-permute-start(bf16[256,512]{1,0:T(8,128)(2,1)} %get-tuple-element.71), channel_id=1, source_target_pairs={{0,4},{2,6},{4,0},{6,2},{8,12},{10,14},{12,8},{14,10},{16,20},{18,... | collective-permute-start | bytes 786440 | tf_op jit(solution)/shard_map/ppermute | solution.py:27
  109.6 46.2 %copy-start.4 = (bf16[1792,512]{1,0:T(8,128)(2,1)S(1)}, bf16[1792,512]{1,0:T(8,128)(2,1)}, u32[]{:S(2)}) copy-start(bf16[1792,512]{1,0:T(8,128)(2,1)} %copy-done.3) | copy-start | bytes 5505028
  109.6 20.1 %collective-permute-start.11 = (bf16[256,512]{1,0:T(8,128)(2,1)}, bf16[256,512]{1,0:T(8,128)(2,1)S(1)}, u32[]{:S(2)}, u32[]{:S(2)}) collective-permute-start(bf16[256,512]{1,0:T(8,128)(2,1)} %get-tuple-element.72), channel_id=1, source_target_pairs={{0,2},{2,0},{4,6},{6,4},{8,10},{10,8},{12,14},{14,12},{16,18},{18,... | collective-permute-start | bytes 786440 | tf_op jit(solution)/shard_map/ppermute | solution.py:27
  130.8 25.1 %copy-start.1 = (bf16[7,512,512]{2,1,0:T(8,128)(2,1)S(1)}, bf16[7,512,512]{2,1,0:T(8,128)(2,1)}, u32[]{:S(2)}) copy-start(bf16[7,512,512]{2,1,0:T(8,128)(2,1)} %refs_6_.7) | copy-start | bytes 11010052
  134.5 21.3 %collective-permute-start.15 = (bf16[4,128,256]{2,1,0:T(8,128)(2,1)S(1)}, bf16[4,128,256]{2,1,0:T(8,128)(2,1)S(1)}, u32[]{:S(2)}, u32[]{:S(2)}) collective-permute-start(bf16[4,128,256]{2,1,0:T(8,128)(2,1)S(1)} %get-tuple-element.35.refs_0_), channel_id=1, source_target_pairs={{0,16},{2,18},{4,20},{6,22},{8,24},{10,26},{12,28},{14,30},{16,0},... | collective-permute-start | bytes 786440 | tf_op jit(solution)/shard_map/ppermute | solution.py:27
  136.0 19.8 %collective-permute-start.16 = (bf16[4,128,256]{2,1,0:T(8,128)(2,1)S(1)}, bf16[4,128,256]{2,1,0:T(8,128)(2,1)S(1)}, u32[]{:S(2)}, u32[]{:S(2)}) collective-permute-start(bf16[4,128,256]{2,1,0:T(8,128)(2,1)S(1)} %get-tuple-element.36), channel_id=1, source_target_pairs={{0,24},{2,26},{4,28},{6,30},{8,16},{10,18},{12,20},{14,22},{16,8},... | collective-permute-start | bytes 786440 | tf_op jit(solution)/shard_map/ppermute | solution.py:27
  138.8 17.0 %collective-permute-start.14 = (bf16[4,128,256]{2,1,0:T(8,128)(2,1)S(1)}, bf16[4,128,256]{2,1,0:T(8,128)(2,1)S(1)}, u32[]{:S(2)}, u32[]{:S(2)}) collective-permute-start(bf16[4,128,256]{2,1,0:T(8,128)(2,1)S(1)} %get-tuple-element.36), channel_id=1, source_target_pairs={{0,8},{2,10},{4,12},{6,14},{8,0},{10,2},{12,4},{14,6},{16,24},{18,... | collective-permute-start | bytes 786440 | tf_op jit(solution)/shard_map/ppermute | solution.py:27
  162.0 115.3 %all-to-all-start = ((bf16[8,224,256]{2,1,0:T(8,128)(2,1)}), bf16[8,224,256]{2,1,0:T(8,128)(2,1)}, u32[]{:S(2)}, u32[]{:S(2)}) async-start(bf16[8,224,256]{2,1,0:T(8,128)(2,1)} %level12.4), calls=%async_computation | async-start | bytes 1835008 | tf_op jit(solution)/shard_map/all_to_all | solution.py:530
  169.4 19.1 %collective-permute-start.33 = (bf16[256,512]{1,0:T(8,128)(2,1)}, bf16[256,512]{1,0:T(8,128)(2,1)S(1)}, u32[]{:S(2)}, u32[]{:S(2)}) collective-permute-start(bf16[256,512]{1,0:T(8,128)(2,1)} %get-tuple-element.64), channel_id=1, source_target_pairs={{0,6},{2,4},{4,2},{6,0},{8,14},{10,12},{12,10},{14,8},{16,22},{18,... | collective-permute-start | bytes 786440 | tf_op jit(solution)/shard_map/ppermute | solution.py:27
  172.3 27.4 %collective-permute-start.32 = (bf16[256,512]{1,0:T(8,128)(2,1)}, bf16[256,512]{1,0:T(8,128)(2,1)S(1)}, u32[]{:S(2)}, u32[]{:S(2)}) collective-permute-start(bf16[256,512]{1,0:T(8,128)(2,1)} %get-tuple-element.65), channel_id=1, source_target_pairs={{0,4},{2,6},{4,0},{6,2},{8,12},{10,14},{12,8},{14,10},{16,20},{18,... | collective-permute-start | bytes 786440 | tf_op jit(solution)/shard_map/ppermute | solution.py:27
  172.9 26.8 %collective-permute-start.31 = (bf16[256,512]{1,0:T(8,128)(2,1)}, bf16[256,512]{1,0:T(8,128)(2,1)S(1)}, u32[]{:S(2)}, u32[]{:S(2)}) collective-permute-start(bf16[256,512]{1,0:T(8,128)(2,1)} %get-tuple-element.66), channel_id=1, source_target_pairs={{0,2},{2,0},{4,6},{6,4},{8,10},{10,8},{12,14},{14,12},{16,18},{18,... | collective-permute-start | bytes 786440 | tf_op jit(solution)/shard_map/ppermute | solution.py:27
  172.9 33.6 %collective-permute-start.20 = (bf16[256,512]{1,0:T(8,128)(2,1)}, bf16[256,512]{1,0:T(8,128)(2,1)S(1)}, u32[]{:S(2)}, u32[]{:S(2)}) collective-permute-start(bf16[256,512]{1,0:T(8,128)(2,1)} %get-tuple-element.67), channel_id=1, source_target_pairs={{0,6},{2,4},{4,2},{6,0},{8,14},{10,12},{12,10},{14,8},{16,22},{18,... | collective-permute-start | bytes 786440 | tf_op jit(solution)/shard_map/ppermute | solution.py:27
  175.8 32.0 %collective-permute-start.19 = (bf16[256,512]{1,0:T(8,128)(2,1)}, bf16[256,512]{1,0:T(8,128)(2,1)S(1)}, u32[]{:S(2)}, u32[]{:S(2)}) collective-permute-start(bf16[256,512]{1,0:T(8,128)(2,1)} %get-tuple-element.68), channel_id=1, source_target_pairs={{0,4},{2,6},{4,0},{6,2},{8,12},{10,14},{12,8},{14,10},{16,20},{18,... | collective-permute-start | bytes 786440 | tf_op jit(solution)/shard_map/ppermute | solution.py:27
  188.5 19.3 %collective-permute-start.18 = (bf16[256,512]{1,0:T(8,128)(2,1)S(1)}, bf16[256,512]{1,0:T(8,128)(2,1)S(1)}, u32[]{:S(2)}, u32[]{:S(2)}) collective-permute-start(bf16[256,512]{1,0:T(8,128)(2,1)S(1)} %get-tuple-element.69), channel_id=1, source_target_pairs={{0,2},{2,0},{4,6},{6,4},{8,10},{10,8},{12,14},{14,12},{16,18},{18,... | collective-permute-start | bytes 786440 | tf_op jit(solution)/shard_map/ppermute | solution.py:27
  204.2 22.4 %collective-permute-start.35 = (bf16[4,128,256]{2,1,0:T(8,128)(2,1)S(1)}, bf16[4,128,256]{2,1,0:T(8,128)(2,1)S(1)}, u32[]{:S(2)}, u32[]{:S(2)}) collective-permute-start(bf16[4,128,256]{2,1,0:T(8,128)(2,1)S(1)} %get-tuple-element.49.refs_0_), channel_id=1, source_target_pairs={{0,16},{2,18},{4,20},{6,22},{8,24},{10,26},{12,28},{14,30},{16,0},... | collective-permute-start | bytes 786440 | tf_op jit(solution)/shard_map/ppermute | solution.py:27
  204.3 22.3 %copy-start.5 = (bf16[1792,512]{1,0:T(8,128)(2,1)S(1)}, bf16[1792,512]{1,0:T(8,128)(2,1)}, u32[]{:S(2)}) copy-start(bf16[1792,512]{1,0:T(8,128)(2,1)} %copy-done.3) | copy-start | bytes 5505028
  204.3 22.3 %collective-permute-start.36 = (bf16[4,128,256]{2,1,0:T(8,128)(2,1)S(1)}, bf16[4,128,256]{2,1,0:T(8,128)(2,1)S(1)}, u32[]{:S(2)}, u32[]{:S(2)}) collective-permute-start(bf16[4,128,256]{2,1,0:T(8,128)(2,1)S(1)} %get-tuple-element.50), channel_id=1, source_target_pairs={{0,24},{2,26},{4,28},{6,30},{8,16},{10,18},{12,20},{14,22},{16,8},... | collective-permute-start | bytes 786440 | tf_op jit(solution)/shard_map/ppermute | solution.py:27
  206.5 20.1 %collective-permute-start.34 = (bf16[4,128,256]{2,1,0:T(8,128)(2,1)S(1)}, bf16[4,128,256]{2,1,0:T(8,128)(2,1)S(1)}, u32[]{:S(2)}, u32[]{:S(2)}) collective-permute-start(bf16[4,128,256]{2,1,0:T(8,128)(2,1)S(1)} %get-tuple-element.50), channel_id=1, source_target_pairs={{0,8},{2,10},{4,12},{6,14},{8,0},{10,2},{12,4},{14,6},{16,24},{18,... | collective-permute-start | bytes 786440 | tf_op jit(solution)/shard_map/ppermute | solution.py:27
  207.8 18.8 %copy-start.2 = (bf16[7,512,512]{2,1,0:T(8,128)(2,1)S(1)}, bf16[7,512,512]{2,1,0:T(8,128)(2,1)}, u32[]{:S(2)}) copy-start(bf16[7,512,512]{2,1,0:T(8,128)(2,1)} %refs_6_.7) | copy-start | bytes 11010052
  211.6 30.5 %collective-permute-start.22 = (bf16[4,128,256]{2,1,0:T(8,128)(2,1)S(1)}, bf16[4,128,256]{2,1,0:T(8,128)(2,1)S(1)}, u32[]{:S(2)}, u32[]{:S(2)}) collective-permute-start(bf16[4,128,256]{2,1,0:T(8,128)(2,1)S(1)} %get-tuple-element.39.refs_0_), channel_id=1, source_target_pairs={{0,16},{2,18},{4,20},{6,22},{8,24},{10,26},{12,28},{14,30},{16,0},... | collective-permute-start | bytes 786440 | tf_op jit(solution)/shard_map/ppermute | solution.py:27
  212.6 30.4 %collective-permute-start.23 = (bf16[4,128,256]{2,1,0:T(8,128)(2,1)S(1)}, bf16[4,128,256]{2,1,0:T(8,128)(2,1)S(1)}, u32[]{:S(2)}, u32[]{:S(2)}) collective-permute-start(bf16[4,128,256]{2,1,0:T(8,128)(2,1)S(1)} %get-tuple-element.40), channel_id=1, source_target_pairs={{0,24},{2,26},{4,28},{6,30},{8,16},{10,18},{12,20},{14,22},{16,8},... | collective-permute-start | bytes 786440 | tf_op jit(solution)/shard_map/ppermute | solution.py:27
  226.6 19.9 %collective-permute-start.21 = (bf16[4,128,256]{2,1,0:T(8,128)(2,1)S(1)}, bf16[4,128,256]{2,1,0:T(8,128)(2,1)S(1)}, u32[]{:S(2)}, u32[]{:S(2)}) collective-permute-start(bf16[4,128,256]{2,1,0:T(8,128)(2,1)S(1)} %get-tuple-element.40), channel_id=1, source_target_pairs={{0,8},{2,10},{4,12},{6,14},{8,0},{10,2},{12,4},{14,6},{16,24},{18,... | collective-permute-start | bytes 786440 | tf_op jit(solution)/shard_map/ppermute | solution.py:27
  232.5 21.0 %collective-permute-start.37 = (bf16[224,256]{1,0:T(8,128)(2,1)}, bf16[224,256]{1,0:T(8,128)(2,1)S(1)}, u32[]{:S(2)}, u32[]{:S(2)}) collective-permute-start(bf16[224,256]{1,0:T(8,128)(2,1)} %get-tuple-element.52), channel_id=1, source_target_pairs={{0,2},{2,0},{4,6},{6,4},{8,10},{10,8},{12,14},{14,12},{16,18},{18,... | collective-permute-start | bytes 344072 | tf_op jit(solution)/shard_map/ppermute | solution.py:27
  232.6 23.1 %collective-permute-start.38 = (bf16[224,256]{1,0:T(8,128)(2,1)}, bf16[224,256]{1,0:T(8,128)(2,1)S(1)}, u32[]{:S(2)}, u32[]{:S(2)}) collective-permute-start(bf16[224,256]{1,0:T(8,128)(2,1)} %get-tuple-element.53), channel_id=1, source_target_pairs={{0,4},{2,6},{4,0},{6,2},{8,12},{10,14},{12,8},{14,10},{16,20},{18,... | collective-permute-start | bytes 344072 | tf_op jit(solution)/shard_map/ppermute | solution.py:27
  242.1 14.4 %collective-permute-start.39 = (bf16[224,256]{1,0:T(8,128)(2,1)}, bf16[224,256]{1,0:T(8,128)(2,1)S(1)}, u32[]{:S(2)}, u32[]{:S(2)}) collective-permute-start(bf16[224,256]{1,0:T(8,128)(2,1)} %get-tuple-element.54), channel_id=1, source_target_pairs={{0,6},{2,4},{4,2},{6,0},{8,14},{10,12},{12,10},{14,8},{16,22},{18,... | collective-permute-start | bytes 344072 | tf_op jit(solution)/shard_map/ppermute | solution.py:27
  243.0 15.0 %collective-permute-start.40 = (bf16[224,256]{1,0:T(8,128)(2,1)}, bf16[224,256]{1,0:T(8,128)(2,1)S(1)}, u32[]{:S(2)}, u32[]{:S(2)}) collective-permute-start(bf16[224,256]{1,0:T(8,128)(2,1)} %get-tuple-element.55), channel_id=1, source_target_pairs={{0,8},{2,10},{4,12},{6,14},{8,0},{10,2},{12,4},{14,6},{16,24},{18,... | collective-permute-start | bytes 344072 | tf_op jit(solution)/shard_map/ppermute | solution.py:27
  246.5 7.1 %copy-start.16 = (bf16[224,256]{1,0:T(8,128)(2,1)S(1)}, bf16[224,256]{1,0:T(8,128)(2,1)}, u32[]{:S(2)}) copy-start(bf16[224,256]{1,0:T(8,128)(2,1)} %get-tuple-element.57) | copy-start | bytes 344068
  246.5 9.2 %copy-start.15 = (bf16[224,256]{1,0:T(8,128)(2,1)S(1)}, bf16[224,256]{1,0:T(8,128)(2,1)}, u32[]{:S(2)}) copy-start(bf16[224,256]{1,0:T(8,128)(2,1)} %get-tuple-element.58) | copy-start | bytes 344068
  246.5 12.2 %collective-permute-start.41 = (bf16[224,256]{1,0:T(8,128)(2,1)}, bf16[224,256]{1,0:T(8,128)(2,1)S(1)}, u32[]{:S(2)}, u32[]{:S(2)}) collective-permute-start(bf16[224,256]{1,0:T(8,128)(2,1)} %get-tuple-element.56), channel_id=1, source_target_pairs={{0,10},{2,8},{4,14},{6,12},{8,2},{10,0},{12,6},{14,4},{16,26},{18,... | collective-permute-start | bytes 344072 | tf_op jit(solution)/shard_map/ppermute | solution.py:27
  253.6 7.5 %collective-permute-start.42 = (bf16[224,256]{1,0:T(8,128)(2,1)S(1)}, bf16[224,256]{1,0:T(8,128)(2,1)S(1)}, u32[]{:S(2)}, u32[]{:S(2)}) collective-permute-start(bf16[224,256]{1,0:T(8,128)(2,1)S(1)} %copy-done.16), channel_id=1, source_target_pairs={{0,12},{2,14},{4,8},{6,10},{8,4},{10,6},{12,0},{14,2},{16,28},{18,... | collective-permute-start | bytes 344072 | tf_op jit(solution)/shard_map/ppermute | solution.py:27
  255.8 6.8 %collective-permute-start.43 = (bf16[224,256]{1,0:T(8,128)(2,1)S(1)}, bf16[224,256]{1,0:T(8,128)(2,1)S(1)}, u32[]{:S(2)}, u32[]{:S(2)}) collective-permute-start(bf16[224,256]{1,0:T(8,128)(2,1)S(1)} %copy-done.15), channel_id=1, source_target_pairs={{0,14},{2,12},{4,10},{6,8},{8,6},{10,4},{12,2},{14,0},{16,30},{18,... | collective-permute-start | bytes 344072 | tf_op jit(solution)/shard_map/ppermute | solution.py:27
  256.5 7.8 %collective-permute-start.24 = (bf16[224,256]{1,0:T(8,128)(2,1)}, bf16[224,256]{1,0:T(8,128)(2,1)S(1)}, u32[]{:S(2)}, u32[]{:S(2)}) collective-permute-start(bf16[224,256]{1,0:T(8,128)(2,1)} %get-tuple-element.42), channel_id=1, source_target_pairs={{0,2},{2,0},{4,6},{6,4},{8,10},{10,8},{12,14},{14,12},{16,18},{18,... | collective-permute-start | bytes 344072 | tf_op jit(solution)/shard_map/ppermute | solution.py:27
  258.1 10.5 %collective-permute-start.25 = (bf16[224,256]{1,0:T(8,128)(2,1)}, bf16[224,256]{1,0:T(8,128)(2,1)S(1)}, u32[]{:S(2)}, u32[]{:S(2)}) collective-permute-start(bf16[224,256]{1,0:T(8,128)(2,1)} %get-tuple-element.43), channel_id=1, source_target_pairs={{0,4},{2,6},{4,0},{6,2},{8,12},{10,14},{12,8},{14,10},{16,20},{18,... | collective-permute-start | bytes 344072 | tf_op jit(solution)/shard_map/ppermute | solution.py:27
  258.8 13.8 %collective-permute-start.26 = (bf16[224,256]{1,0:T(8,128)(2,1)}, bf16[224,256]{1,0:T(8,128)(2,1)S(1)}, u32[]{:S(2)}, u32[]{:S(2)}) collective-permute-start(bf16[224,256]{1,0:T(8,128)(2,1)} %get-tuple-element.44), channel_id=1, source_target_pairs={{0,6},{2,4},{4,2},{6,0},{8,14},{10,12},{12,10},{14,8},{16,22},{18,... | collective-permute-start | bytes 344072 | tf_op jit(solution)/shard_map/ppermute | solution.py:27
  261.1 11.5 %collective-permute-start.27 = (bf16[224,256]{1,0:T(8,128)(2,1)}, bf16[224,256]{1,0:T(8,128)(2,1)S(1)}, u32[]{:S(2)}, u32[]{:S(2)}) collective-permute-start(bf16[224,256]{1,0:T(8,128)(2,1)} %get-tuple-element.45), channel_id=1, source_target_pairs={{0,8},{2,10},{4,12},{6,14},{8,0},{10,2},{12,4},{14,6},{16,24},{18,... | collective-permute-start | bytes 344072 | tf_op jit(solution)/shard_map/ppermute | solution.py:27
  262.6 10.0 %collective-permute-start.28 = (bf16[224,256]{1,0:T(8,128)(2,1)}, bf16[224,256]{1,0:T(8,128)(2,1)S(1)}, u32[]{:S(2)}, u32[]{:S(2)}) collective-permute-start(bf16[224,256]{1,0:T(8,128)(2,1)} %get-tuple-element.46), channel_id=1, source_target_pairs={{0,10},{2,8},{4,14},{6,12},{8,2},{10,0},{12,6},{14,4},{16,26},{18,... | collective-permute-start | bytes 344072 | tf_op jit(solution)/shard_map/ppermute | solution.py:27
  264.3 8.3 %collective-permute-start.29 = (bf16[224,256]{1,0:T(8,128)(2,1)}, bf16[224,256]{1,0:T(8,128)(2,1)S(1)}, u32[]{:S(2)}, u32[]{:S(2)}) collective-permute-start(bf16[224,256]{1,0:T(8,128)(2,1)} %get-tuple-element.47), channel_id=1, source_target_pairs={{0,12},{2,14},{4,8},{6,10},{8,4},{10,6},{12,0},{14,2},{16,28},{18,... | collective-permute-start | bytes 344072 | tf_op jit(solution)/shard_map/ppermute | solution.py:27
  268.6 2.3 copy-start.13
  268.6 7.1 %collective-permute-start.30 = (bf16[224,256]{1,0:T(8,128)(2,1)}, bf16[224,256]{1,0:T(8,128)(2,1)S(1)}, u32[]{:S(2)}, u32[]{:S(2)}) collective-permute-start(bf16[224,256]{1,0:T(8,128)(2,1)} %get-tuple-element.48), channel_id=1, source_target_pairs={{0,14},{2,12},{4,10},{6,8},{8,6},{10,4},{12,2},{14,0},{16,30},{18,... | collective-permute-start | bytes 344072 | tf_op jit(solution)/shard_map/ppermute | solution.py:27
  270.9 4.7 %copy-start.14 = (bf16[224,256]{1,0:T(8,128)(2,1)S(1)}, bf16[224,256]{1,0:T(8,128)(2,1)}, u32[]{:S(2)}) copy-start(bf16[224,256]{1,0:T(8,128)(2,1)} %get-tuple-element.41.refs_0_) | copy-start | bytes 344068
  (5 other events, 5.6 us)
